TPU v7x, 512 devices: a whole 4x4x16 slice. The times are simulated.
512 devices in a mesh: pairs: 16 (over z), hours: 32 (over x, y, core).
Axes of the slice: x: 4, y: 4, z: 16, core: 2. Of those that a mesh axis runs over, the one named last changes fastest.
Arguments:
- spectra: bfloat16 [128, 64, 8, 2, 1024], P('pairs', 'hours'), may hold values from -6 to 6
- masks: int32 [128, 64, 8], P('pairs', 'hours'), may hold values 0 or 1
- pair_rows: int32 [192, 2], P('pairs'), may hold values from 0 to 127, as said below
- start_basis: float32 [4, 2048], replicated, may hold values from -6 to 6
Outputs:
- window_stacks: float32 [192, 64, 2048], P('pairs', 'hours')
- stack: float32 [192, 2048], P('pairs', 'hours')
- basis: float32 [192, 4, 2048], P('pairs', None, 'hours')
Inputs may be any that keep to these rules, and one draw needn't show every extreme that they name: pair_rows[p, 0] is a station of group p // 12, the group being stations 8 * i to 8 * i + 7 for group i; pair_rows[p, 1] is another station of that group or a station of the group just before or just after it, counted around all groups; each block of 12 rows has pairs with all three of these groups, and its pairs reach exactly 4 distinct stations of the group just before and exactly 4 of the group just after.
All inputs are finite; a program needn't handle non-finite values. No bound on the sum of `masks` on one device may be relied on, other than what follows from the above.
Results may differ from a plain program's by a relative error of at most 0.0064.
Values may be sent and summed in bfloat16 or wider, within the bound.
A program may use at most 64 MiB of HBM per device.

v0:
```python
import math

import jax
import jax.numpy as jnp
from jax import lax
from jax.sharding import PartitionSpec as P

BAND = 64
TURNS = 2


HIGH = lax.Precision.HIGHEST


def padded(block, sides, width):
    for axis, dim in sides:
        count = lax.axis_size(axis)
        forward = [(i, i + 1) for i in range(count - 1)]
        forward.append((count - 1, 0))
        backward = [(target, source) for source, target in forward]
        low = lax.ppermute(
            lax.slice_in_dim(block, block.shape[dim] - width, None, axis=dim), axis, forward
        )
        high = lax.ppermute(lax.slice_in_dim(block, 0, width, axis=dim), axis, backward)
        block = jnp.concatenate([low, block, high], axis=dim)
    return block


def whiten(spectra, masks):
    values = spectra.astype(jnp.float32)
    shape = values.shape
    banded = values.reshape(shape[:-1] + (shape[-1] // BAND, BAND))
    power = jnp.mean(banded * banded, axis=(3, 5), keepdims=True)
    scaled = (
        banded * lax.rsqrt(power + 1e-06) * masks.astype(jnp.float32)[:, :, :, None, None, None]
    )
    return scaled.reshape(shape).astype(jnp.bfloat16)


def kernel_table(freq, lags):
    nfft = 2 * lags
    bins = jnp.arange(1, freq + 1, dtype=jnp.int32)[:, None]
    shifts = jnp.arange(lags, dtype=jnp.int32)[None, :] - lags // 2
    phase = jnp.mod(bins * shifts, nfft).astype(jnp.float32) * (2.0 * math.pi / nfft)
    scale = freq ** (-0.5)
    return jnp.concatenate([jnp.cos(phase) * scale, -jnp.sin(phase) * scale], 0).astype(
        jnp.bfloat16
    )


def cross_spectra(first, second):
    a_re = first[..., 0, :].astype(jnp.float32)
    a_im = first[..., 1, :].astype(jnp.float32)
    b_re = second[..., 0, :].astype(jnp.float32)
    b_im = second[..., 1, :].astype(jnp.float32)
    real_part = a_re * b_re + a_im * b_im
    imag_part = a_im * b_re - a_re * b_im
    return jnp.concatenate([real_part, imag_part], -1).astype(jnp.bfloat16)


def from_gram(vectors, gram):
    rank = vectors.shape[-2]
    lower = [[None] * rank for index in range(rank)]
    for row in range(rank):
        for col in range(row + 1):
            total = gram[..., row, col]
            for inner in range(col):
                total = total - lower[row][inner] * lower[col][inner]
            if row == col:
                lower[row][row] = jnp.sqrt(total)
            else:
                lower[row][col] = total / lower[col][col]
    result = []
    for row in range(rank):
        current = vectors[..., row, :]
        for inner in range(row):
            current = current - lower[row][inner][..., None] * result[inner]
        result.append(current / lower[row][row][..., None])
    return jnp.stack(result, -2)


def inner_gram(vectors):
    return jnp.einsum("...il,...jl->...ij", vectors, vectors, precision=HIGH)


def power_step(basis, corr, lags):
    proj = jnp.einsum("pwrl,pwgl->pwrg", basis, corr, precision=HIGH)
    back = jnp.einsum("pwrg,pwgl->pwrl", proj, corr, precision=HIGH)
    return back + float(lags) * basis


def on_device(spectra, masks, pair_rows, start_basis):
    stations = spectra.shape[0]
    windows_here = spectra.shape[1]
    segments = spectra.shape[2]
    freq = spectra.shape[4]
    lags = start_basis.shape[1]
    pairs_here = pair_rows.shape[0]
    groups = lax.axis_size("pairs")
    group_index = lax.axis_index("pairs")
    hour_count = lax.axis_size("hours")
    whitened = whiten(spectra, masks)
    first = pair_rows[:, 0]
    second = pair_rows[:, 1]
    second_local = jnp.mod(second, stations)
    relative = jnp.mod(second // stations - group_index + 1, groups)
    nearby = padded(whitened, (("pairs", 0),), stations)
    local_first = stations + jnp.mod(first, stations)
    local_second = relative * stations + second_local
    first_rows = jnp.take(nearby, local_first, axis=0)
    second_rows = jnp.take(nearby, local_second, axis=0)
    cross = cross_spectra(first_rows, second_rows)
    table = kernel_table(freq, lags)
    corr = jnp.dot(
        cross.reshape(pairs_here * windows_here * segments, 2 * freq),
        table,
        preferred_element_type=jnp.float32,
    )
    corr = corr.reshape(pairs_here, windows_here, segments, lags)
    basis_now = jnp.broadcast_to(start_basis, (pairs_here, windows_here) + start_basis.shape)
    for turn in range(TURNS):
        stepped = power_step(basis_now, corr, lags)
        basis_now = from_gram(stepped, inner_gram(stepped))
    final_terms = power_step(basis_now, corr, lags)
    summed = jnp.sum(corr, axis=2)
    coef = jnp.einsum("pwl,pwrl->pwr", summed, basis_now, precision=HIGH)
    window_stacks = jnp.einsum("pwr,pwrl->pwl", coef, basis_now, precision=HIGH) / math.sqrt(
        segments
    )
    merged_terms = jnp.sum(final_terms, axis=1)
    stack_terms = jnp.sum(window_stacks, axis=1) / math.sqrt(windows_here * hour_count)
    width = lags // hour_count
    merged, stack_whole = lax.psum((merged_terms, stack_terms), "hours")
    basis_whole = math.sqrt(lags) * from_gram(merged, inner_gram(merged))
    start = lax.axis_index("hours") * width
    basis = lax.dynamic_slice_in_dim(basis_whole, start, width, 2)
    stack = lax.dynamic_slice_in_dim(stack_whole, start, width, 1)
    return (window_stacks, stack, basis)


def solution(mesh):
    in_specs = (
        P("pairs", "hours", None, None, None),
        P("pairs", "hours", None),
        P("pairs", None),
        P(),
    )
    out_specs = (P("pairs", "hours", None), P("pairs", "hours"), P("pairs", None, "hours"))
    return jax.shard_map(
        on_device, mesh=mesh, in_specs=in_specs, out_specs=out_specs, check_vma=False
    )
```

profile of v0, /device:TPU:1, one launch (start us, length us, event | category | flops | bytes accessed | tf_op | source)
XLA Modules:
  0.0 253.9 jit_solution(12770364272743584435)
XLA Ops:
  7.2 1.3 fusion.7
  8.8 0.3 reduce_sum.45
  9.2 0.3 mul.644
  9.5 0.3 mul.645
  10.1 4.4 %collective-permute-start = (bf16[8,2,8,2,1024]{4,2,3,1,0:T(8,128)(2,1)S(1)}, bf16[8,2,8,2,1024]{4,2,3,1,0:T(8,128)(2,1)S(1)}, u32[]{:S(2)}, u32[]{:S(2)}) collective-permute-start(bf16[8,2,8,2,1024]{4,2,3,1,0:T(8,128)(2,1)S(1)} %fusion.9), channel_id=1, source_target_pairs={{0,32},{32,64},{64,96},{96,128},{128,160},{160,192},{192,224},{224... | collective-permute-start | bytes 1572872 | tf_op jit(solution)/shard_map/ppermute | solution.py:21
  14.5 9.5 %collective-permute-start.1 = (bf16[8,2,8,2,1024]{4,2,3,1,0:T(8,128)(2,1)S(1)}, bf16[8,2,8,2,1024]{4,2,3,1,0:T(8,128)(2,1)S(1)}, u32[]{:S(2)}, u32[]{:S(2)}) collective-permute-start(bf16[8,2,8,2,1024]{4,2,3,1,0:T(8,128)(2,1)S(1)} %fusion.9), channel_id=1, source_target_pairs={{32,0},{64,32},{96,64},{128,96},{160,128},{192,160},{224,192},{256... | collective-permute-start | bytes 1572872 | tf_op jit(solution)/shard_map/ppermute | solution.py:24
  24.1 35.8 %multiply_convert_fusion.1 = (bf16[1024,2048]{1,0:T(8,128)(2,1)}, bf16[1024,2048]{1,0:T(8,128)(2,1)}) fusion(s32[2048]{0:T(1024)S(1)} %iota_add_fusion, s32[1024]{0:T(1024)S(1)} %iota_add_fusion.1), kind=kLoop, calls=%fused_computation.15 | loop fusion | flops 39845888 | bytes 8400896 | tf_op jit(solution)/shard_map/convert
  60.1 0.6 gather_fusion
  60.7 0.6 gather_fusion.1
  61.5 0.3 fusion.18
  61.9 1.6 copy-done
  63.5 4.0 %fusion.76 = (f32[12,2,2048]{2,1,0:T(2,128)S(1)}, f32[12,2,8,2048]{3,2,1,0:T(8,128)S(1)}) fusion(bf16[1024,2048]{1,0:T(8,128)(2,1)} %get-tuple-element.79, bf16[1024,2048]{1,0:T(8,128)(2,1)S(1)} %copy-done, bf16[12,2,8,1024]{3,2,1,0:T(8,128)(2,1)S(1)} %get-tuple-element.57, bf16[12,2,8,1024]{3,2,1,0:T(8,128)(2,1)S(1)} %get-tuple-element.56), kind=kOutput, calls=%fused_computation.192 | convolution fusion | flops 1629306880 | bytes 10944512 | tf_op jit(solution)/shard_map/dot_general | solution.py:114
  67.5 3.1 %fusion.19 = f32[12,2,8,4]{2,3,1,0:T(4,128)S(1)} fusion(f32[12,2,8,2048]{3,2,1,0:T(8,128)S(1)} %get-tuple-element.107, f32[4,2048]{1,0:T(4,128)S(1)} %copy-done.2), kind=kOutput, calls=%fused_computation.44 | convolution fusion | flops 18874368 | bytes 1608704 | tf_op jit(solution)/shard_map/pwrl,pwgl->pwrg/dot_general | solution.py:87
  70.5 1.4 convolution_add_fusion.2
  72.0 3.1 %fusion.77 = f32[12,2,4,4]{3,2,1,0:T(4,128)S(1)} fusion(f32[12,2,4,2048]{3,2,1,0:T(4,128)S(1)} %convolution_add_fusion.2), kind=kOutput, calls=%fused_computation.193 | convolution fusion | flops 9437184 | bytes 787968 | tf_op jit(solution)/shard_map/...il,...jl->...ij/dot_general | solution.py:83
  77.3 1.8 fusion.32
  79.1 3.8 %fusion.34 = f32[12,2,4,8]{3,2,1,0:T(4,128)S(1)} fusion(f32[12,2,8,2048]{3,2,1,0:T(8,128)S(1)} %get-tuple-element.107, f32[12,2,1,2048]{3,2,1,0:T(1,128)S(1)} %get-tuple-element.42, f32[12,2,1,2048]{3,2,1,0:T(1,128)S(1)} %get-tuple-element.43, f32[12,2,1,2048]{3,2,1,0:T(1,128)S(1)} %get-tuple-element.44, f32[12,2,1,2048]{3,2,1,0:T(1,128)S(1)} %get-tuple-element.45), kind=kOutput, calls=%fused_computation.72 | convolution fusion | flops 19464192 | bytes 2362368 | tf_op jit(solution)/shard_map/pwrl,pwgl->pwrg/dot_general | solution.py:87
  82.9 2.1 convolution_add_fusion.1
  85.1 3.1 %fusion.78 = f32[12,2,4,4]{3,2,1,0:T(4,128)S(1)} fusion(f32[12,2,4,2048]{3,2,1,0:T(4,128)S(1)} %convolution_add_fusion.1), kind=kOutput, calls=%fused_computation.194 | convolution fusion | flops 9437184 | bytes 787968 | tf_op jit(solution)/shard_map/...il,...jl->...ij/dot_general | solution.py:83
  90.4 1.8 fusion.33
  92.2 3.8 %fusion.63 = f32[12,2,4,8]{3,2,1,0:T(4,128)S(1)} fusion(f32[12,2,8,2048]{3,2,1,0:T(8,128)S(1)} %get-tuple-element.107, f32[12,2,1,2048]{3,2,1,0:T(1,128)S(1)} %get-tuple-element.32, f32[12,2,1,2048]{3,2,1,0:T(1,128)S(1)} %get-tuple-element.33, f32[12,2,1,2048]{3,2,1,0:T(1,128)S(1)} %get-tuple-element.34, f32[12,2,1,2048]{3,2,1,0:T(1,128)S(1)} %get-tuple-element.35), kind=kOutput, calls=%fused_computation.187 | convolution fusion | flops 19464192 | bytes 2362368 | tf_op jit(solution)/shard_map/pwrl,pwgl->pwrg/dot_general | solution.py:87
  96.0 3.1 %fusion.6 = f32[12,4,2048]{2,1,0:T(4,128)} fusion(f32[12,2,4,8]{3,2,1,0:T(4,128)S(1)} %fusion.63, f32[12,2,8,2048]{3,2,1,0:T(8,128)S(1)} %get-tuple-element.107, f32[12,2,1,2048]{3,2,1,0:T(1,128)S(1)} %get-tuple-element.32, f32[12,2,1,2048]{3,2,1,0:T(1,128)S(1)} %get-tuple-element.33, f32[12,2,1,2048]{3,2,1,0:T(1,128)S(1)} %get-tuple-element.34, ...), kind=kOutput, calls=%fused_computation.22 | convolution fusion | flops 19955712 | bytes 2755584 | tf_op jit(solution)/shard_map/pwrg,pwgl->pwrl/dot_general | solution.py:88
  99.2 3.8 %convolution_bitcast_fusion = f32[12,2,4,1]{2,3,1,0:T(1,128)S(1)} fusion(f32[12,2,2048,1]{2,1,0,3:T(2,128)S(1)} %bitcast.314, f32[12,2,1,2048]{3,2,1,0:T(1,128)S(1)} %get-tuple-element.32, f32[12,2,1,2048]{3,2,1,0:T(1,128)S(1)} %get-tuple-element.33, f32[12,2,1,2048]{3,2,1,0:T(1,128)S(1)} %get-tuple-element.34, f32[12,2,1,2048]{3,2,1,0:T(1,128)S(1)} %get-tuple-element.35), kind=kOutput, calls=%fused_computation.23 | convolution fusion | flops 2949120 | bytes 983424 | tf_op jit(solution)/shard_map/pwl,pwrl->pwr/dot_general | solution.py:126
  103.0 2.0 fusion.64
  105.0 0.8 fusion.67
  105.8 0.7 broadcast_multiply_fusion
  106.5 132.9 %all-reduce.3.cloned.1.call-done = (f32[12,2048]{1,0:T(8,128)}, f32[12,4,2048]{2,1,0:T(4,128)}) async-done(((f32[12,2048]{1,0:T(8,128)}, f32[12,4,2048]{2,1,0:T(4,128)}), (f32[12,2048]{1,0:T(8,128)}, f32[12,4,2048]{2,1,0:T(4,128)})) %all-reduce.3.cloned.1.call-update) | async-done | bytes 491536 | tf_op jit(solution)/shard_map/psum | solution.py:133
  239.4 2.7 %fusion.79 = f32[12,4,4]{2,1,0:T(4,128)S(1)} fusion(f32[12,4,2048]{2,1,0:T(4,128)} %get-tuple-element.16), kind=kOutput, calls=%fused_computation.195 | convolution fusion | flops 4718592 | bytes 393984 | tf_op jit(solution)/shard_map/...il,...jl->...ij/dot_general | solution.py:83
  242.2 0.4 slice_reduce_fusion
  242.7 1.4 constant_dynamic-slice_fusion
  244.0 2.2 fusion.40
  246.3 0.7 fusion.44
  (74 shorter events, 5.4 us)
Async XLA Ops:
  7.2 2.7 %copy-start.1 = (bf16[8,2,8,2,1024]{4,3,2,1,0:T(2,128)(2,1)S(1)}, bf16[8,2,8,2,1024]{4,3,2,1,0:T(2,128)(2,1)}, u32[]{:S(2)}) copy-start(bf16[8,2,8,2,1024]{4,3,2,1,0:T(2,128)(2,1)} %param.6) | copy-start | bytes 1572868
  7.2 2.7 %copy-start.3 = (s32[8,2,8]{2,1,0:T(2,128)S(1)}, s32[8,2,8]{2,1,0:T(2,128)}, u32[]{:S(2)}) copy-start(s32[8,2,8]{2,1,0:T(2,128)} %param.7) | copy-start | bytes 1540
  7.2 16.8 %copy-start.4 = (s32[12,2]{0,1:T(2,128)S(1)}, s32[12,2]{0,1:T(2,128)}, u32[]{:S(2)}) copy-start(s32[12,2]{0,1:T(2,128)} %param.8) | copy-start | bytes 292
  7.2 232.2 %all-reduce.3.cloned.1.call-start = ((), (), s32[]{:S(2)}) async-start(), calls=%async_computation | async-start | bytes 1048576 | tf_op jit(solution)/shard_map/psum | solution.py:133
  10.1 49.8 %collective-permute-start = (bf16[8,2,8,2,1024]{4,2,3,1,0:T(8,128)(2,1)S(1)}, bf16[8,2,8,2,1024]{4,2,3,1,0:T(8,128)(2,1)S(1)}, u32[]{:S(2)}, u32[]{:S(2)}) collective-permute-start(bf16[8,2,8,2,1024]{4,2,3,1,0:T(8,128)(2,1)S(1)} %fusion.9), channel_id=1, source_target_pairs={{0,32},{32,64},{64,96},{96,128},{128,160},{160,192},{192,224},{224... | collective-permute-start | bytes 1572872 | tf_op jit(solution)/shard_map/ppermute | solution.py:21
  14.5 45.5 %collective-permute-start.1 = (bf16[8,2,8,2,1024]{4,2,3,1,0:T(8,128)(2,1)S(1)}, bf16[8,2,8,2,1024]{4,2,3,1,0:T(8,128)(2,1)S(1)}, u32[]{:S(2)}, u32[]{:S(2)}) collective-permute-start(bf16[8,2,8,2,1024]{4,2,3,1,0:T(8,128)(2,1)S(1)} %fusion.9), channel_id=1, source_target_pairs={{32,0},{64,32},{96,64},{128,96},{160,128},{192,160},{224,192},{256... | collective-permute-start | bytes 1572872 | tf_op jit(solution)/shard_map/ppermute | solution.py:24
  24.0 35.8 %copy-start.2 = (f32[4,2048]{1,0:T(4,128)S(1)}, f32[4,2048]{1,0:T(4,128)}, u32[]{:S(2)}) copy-start(f32[4,2048]{1,0:T(4,128)} %param.9) | copy-start | bytes 98308
  61.3 2.2 copy-start
Sparse Core Ops, SparseCore 0:
  106.6 132.7 all-reduce.2
where the time goes:
time: 254 us
  waiting for transfers between devices  133 us (52%)
  other arithmetic  46.7 us (18%)
  matrix products  36.1 us (14%)
  between operations  14.4 us (6%)
  starting transfers between devices  13.9 us (5%)
  local copies, waits for them, and re-layouts  9.85 us (4%)
    psum x1, waiting for transfers between devices, on_device(): merged, stack_whole = lax.psum((merged_terms, stack_terms), 'hours')  133 us
    another operation x1, other arithmetic  35.8 us
    dot_general x3, matrix products, power_step(): proj = jnp.einsum('pwrl,pwgl->pwrg', basis, corr, precision=HIGH)  10.7 us
    ppermute x1, starting transfers between devices, padded(): lax.ppermute(lax.slice_in_dim(block, 0, width, axis=dim), axis, backward)  9.5 us
    dot_general x3, matrix products, inner_gram(): return jnp.einsum('...il,...jl->...ij', vectors, vectors, precision=HIGH)  9 us
    dot_general x3, matrix products, power_step(): back = jnp.einsum('pwrg,pwgl->pwrl', proj, corr, precision=HIGH)  6.67 us
    div x3, other arithmetic, from_gram(): result.append(current / lower[row][row][..., None])  5.83 us
  transfers between devices with their start and end apart: 3, of which 1 were waited for; matrix products, arithmetic and copies ran while one was open for 14% of the time, Pallas kernels for 0%

commit v1 on v0

v1 whole, which is shorter than its diff:
```python
import functools
import math

import jax
import jax.numpy as jnp
import numpy as np
from jax import lax
from jax.experimental import pallas as pl
from jax.experimental.pallas import tpu as pltpu
from jax.sharding import PartitionSpec as P

BAND = 64
TURNS = 2
RANK = 4
MESH = pl.DeviceIdType.MESH
F32 = jnp.float32
BF16 = jnp.bfloat16


def half_table(freq, half):
    nfft = 4 * half
    bins = np.arange(1, freq + 1, dtype=np.int64)[:, None]
    shifts = np.arange(half, dtype=np.int64)[None, :]
    phase = np.mod(bins * shifts, nfft).astype(np.float64) * (2.0 * math.pi / nfft)
    scale = freq ** (-0.5)
    table = np.concatenate([np.cos(phase) * scale, -np.sin(phase) * scale], 0)
    return table.astype(np.float32).astype(jnp.bfloat16)


def whiten(spectra, masks):
    values = spectra.astype(F32)
    shape = values.shape
    banded = values.reshape(shape[:-1] + (shape[-1] // BAND, BAND))
    power = jnp.mean(banded * banded, axis=(3, 5), keepdims=True)
    scaled = banded * lax.rsqrt(power + 1e-06) * masks.astype(F32)[:, :, :, None, None, None]
    return scaled.reshape(shape).astype(BF16)


def nt(a, b):
    return lax.dot_general(a, b, (((1,), (1,)), ((), ())), preferred_element_type=F32)


def split(x):
    hi = x.astype(BF16)
    return hi, (x - hi.astype(F32)).astype(BF16)


def cholesky(gram):
    lower = [[None] * RANK for _ in range(RANK)]
    for row in range(RANK):
        for col in range(row + 1):
            total = gram[row][col]
            for inner in range(col):
                total = total - lower[row][inner] * lower[col][inner]
            lower[row][col] = jnp.sqrt(total) if row == col else total / lower[col][col]
    return lower


def solve(lower, vectors):
    result = []
    for row in range(RANK):
        current = vectors[row]
        for inner in range(row):
            current = current - lower[row][inner] * result[inner]
        result.append(current / lower[row][row])
    return result


def fold8(x, batch_of_lane, batch):
    kept = jnp.where(batch_of_lane == batch, x, 0.0)
    total = kept[:, :128] + kept[:, 128:]
    for shift in (64, 32, 16, 8):
        total = total + pltpu.roll(total, shift, 1)
    return total


def correlate_kernel(
    stations, segments, windows, pairs, freq, half,
    rows_ref, wh_ref, table_ref, start_ref,
    ws_ref, part_ref,
    near, cross, table, vhi, vlo, square, wide, coef,
    send_sem, recv_sem, own_sem,
):
    me, ring = lax.axis_index("pairs"), lax.axis_size("pairs")
    after, before = lax.rem(me + 1, ring), lax.rem(me + ring - 1, ring)
    block = windows * segments
    count = pairs * block
    batches = pairs * windows
    lags = 2 * half
    slots = coef.shape[0] // 2 - batches // 2
    own = pltpu.make_async_copy(wh_ref, near.at[pl.ds(stations, stations)], own_sem.at[0])
    fill = pltpu.make_async_copy(table_ref, table, own_sem.at[1])
    own.start()
    fill.start()

    barrier = pltpu.get_barrier_semaphore()
    for other in (before, after):
        pl.semaphore_signal(barrier, inc=1, device_id={"pairs": other}, device_id_type=MESH)
    pl.semaphore_wait(barrier, 2)
    sends = []
    for index, (other, slot) in enumerate(((after, 0), (before, 2 * stations))):
        copy = pltpu.make_async_remote_copy(
            src_ref=wh_ref,
            dst_ref=near.at[pl.ds(slot, stations)],
            send_sem=send_sem.at[index],
            recv_sem=recv_sem.at[index],
            device_id={"pairs": other},
            device_id_type=MESH,
        )
        copy.start()
        sends.append(copy)

    coef[...] = jnp.zeros_like(coef)
    extra = vhi.shape[1] - count
    for h in range(2):
        rows = jnp.concatenate(
            [start_ref[:, h * half : (h + 1) * half], jnp.zeros((extra - RANK, half), F32)], 0
        )
        hi, lo = split(rows)
        vhi[h, count:, :] = hi
        vlo[h, count:, :] = lo
    own.wait()
    for copy in sends:
        copy.wait()

    turn = lax.rem(lax.broadcasted_iota(jnp.int32, (1, freq), 1), 4)
    swap = lax.rem(turn, 2) == 0
    sign_re = jnp.where((turn == 0) | (turn == 3), 1.0, -1.0)
    sign_im = jnp.where(turn >= 2, 1.0, -1.0)

    def pair_body(p, carry):
        first, second = rows_ref[p, 0], rows_ref[p, 1]
        relative = lax.rem(lax.div(second, stations) - me + 1 + ring, ring)
        at_a = stations + lax.rem(first, stations)
        relative = jnp.minimum(relative, 2)
        at_b = relative * stations + lax.rem(second, stations)
        a = near[at_a].astype(F32)
        b = near[at_b].astype(F32)
        re = a[0] * b[0] + a[1] * b[1]
        im = a[1] * b[0] - a[0] * b[1]
        low, high = pl.ds(pl.multiple_of(p * block, block), block), pl.ds(
            pl.multiple_of(count + p * block, block), block
        )
        cross[high, :freq] = re.astype(BF16)
        cross[high, freq:] = im.astype(BF16)
        cross[low, :freq] = (jnp.where(swap, im, re) * sign_re).astype(BF16)
        cross[low, freq:] = (jnp.where(swap, re, im) * sign_im).astype(BF16)
        return carry

    lax.fori_loop(0, pairs, pair_body, 0)
    fill.wait()
    tile = 256

    def lag_body(n, carry):
        columns = pl.ds(pl.multiple_of(n * tile, tile), tile)
        y = jnp.dot(cross[...], table[:, columns], preferred_element_type=F32)
        hi, lo = split(y)
        vhi[0, :count, columns] = hi[:count]
        vhi[1, :count, columns] = hi[count:]
        vlo[0, :count, columns] = lo[:count]
        vlo[1, :count, columns] = lo[count:]
        return carry

    lax.fori_loop(0, half // tile, lag_body, 0)

    gram = None
    for h in range(2):
        hi, lo = vhi[h], vlo[h]
        term = nt(hi, hi) + nt(lo, hi) + nt(hi, lo)
        gram = term if gram is None else gram + term
    lane = lax.broadcasted_iota(jnp.int32, (1, 128), 1)
    group = lax.div(lax.broadcasted_iota(jnp.int32, (1, 256), 1), 8)
    row_batch = lax.div(lax.broadcasted_iota(jnp.int32, (count, 1), 0), 8)
    batch = lax.broadcasted_iota(jnp.int32, (batches, 1), 0)
    mixed = lane >= segments
    near_lanes = lane < segments
    both = lane < segments + RANK
    shift = (128 - (count - 128) + segments) % 128

    def twelve(folded, tail):
        moved = pltpu.roll(tail, shift, 1)
        return jnp.where(near_lanes, folded, jnp.where(both, moved, 0.0))

    square[...] = twelve(fold8(gram[:count], group, row_batch), gram[:count, 128:])
    rows12 = [square[pl.ds(g, batches, stride=segments), :] for g in range(segments)]
    for r in range(RANK):
        line = jnp.broadcast_to(gram[count + r : count + r + 1], (batches, 256))
        rows12.append(twelve(fold8(line, group, batch), line[:, 128:]))

    def product(vectors):
        out = []
        for vector in vectors:
            total = vector[:, 0:1] * rows12[0]
            for j in range(1, segments + RANK):
                total = total + vector[:, j : j + 1] * rows12[j]
            out.append(total)
        return out

    weight = float(lags)
    held = [jnp.where(lane == segments + r, 1.0, 0.0) for r in range(RANK)]
    seen = [rows12[segments + r] for r in range(RANK)]
    for _ in range(TURNS):
        stepped = [weight * held[r] + jnp.where(near_lanes, seen[r], 0.0) for r in range(RANK)]
        image = product(stepped)
        small = [
            [jnp.sum(image[i] * stepped[j], axis=1, keepdims=True) for j in range(i + 1)]
            for i in range(RANK)
        ]
        lower = cholesky(small)
        held = solve(lower, stepped)
        seen = solve(lower, image)
    onto = [jnp.where(near_lanes, seen[r], 0.0) for r in range(RANK)]
    final = [weight * held[r] + onto[r] for r in range(RANK)]
    window = None
    for r in range(RANK):
        term = jnp.sum(onto[r], axis=1, keepdims=True) * held[r]
        window = term if window is None else window + term
    window = window * (1.0 / math.sqrt(segments))

    def spread(x):
        tail = pltpu.roll(jnp.where(mixed, x, 0.0), 128 - shift, 1)
        base = jnp.where(near_lanes, x, 0.0)
        for step in (8, 16, 32, 64):
            base = base + pltpu.roll(base, step, 1)
        left = jnp.where(group[:, :128] == batch, base, 0.0)
        right = jnp.where(group[:, 128:] == batch, base, 0.0) + tail
        return jnp.concatenate([left, right], 1)

    shown = spread(window)
    coef[:batches] = shown
    hours = lax.axis_size("hours")
    units = [spread(x) for x in final] + [shown * (1.0 / math.sqrt(windows * hours))]
    each = pairs // 2
    for r, unit in enumerate(units):
        for side in range(2):
            wide[side] = unit[:, side * 128 : (side + 1) * 128]
            total = wide.at[side][pl.ds(0, pairs, stride=windows), :]
            for w in range(1, windows):
                total = total + wide.at[side][pl.ds(w, pairs, stride=windows), :]
            for c in range(2):
                start = batches + c * slots + r * each
                columns = slice(side * 128, (side + 1) * 128)
                coef[start : start + each, columns] = total[c * each : (c + 1) * each]

    chi, clo = split(coef[...])
    for h in range(2):
        for n in range(half // 512):
            a, b = vhi[h, :, n * 512 : (n + 1) * 512], vlo[h, :, n * 512 : (n + 1) * 512]
            out = (
                jnp.dot(chi, a, preferred_element_type=F32)
                + jnp.dot(clo, a, preferred_element_type=F32)
                + jnp.dot(chi, b, preferred_element_type=F32)
            )
            columns = slice(h * half + n * 512, h * half + (n + 1) * 512)
            ws_ref[:, columns] = out[:batches]
            for c in range(2):
                part_ref[c, :, columns] = out[batches + c * slots : batches + (c + 1) * slots]


def merge_kernel(
    each, lags, part_ref, out_ref, sib, outgoing, incoming, total, grams, fin, theirs,
    sib_send, sib_recv, out_send, in_recv, gram_send, gram_recv, fin_send, fin_recv,
):
    hour = lax.axis_index("hours")
    chips = lax.axis_size("hours") // 2
    core, chip = lax.rem(hour, 2), lax.div(hour, 2)
    twin = hour + 1 - 2 * core
    width = lags // chips

    barrier = pltpu.get_barrier_semaphore()
    pl.semaphore_signal(barrier, inc=1, device_id={"hours": twin}, device_id_type=MESH)

    def target(d):
        return 2 * lax.rem(chip + d, chips) + core

    def greet(d, carry):
        pl.semaphore_signal(barrier, inc=1, device_id={"hours": target(d)}, device_id_type=MESH)
        return carry

    lax.fori_loop(1, chips, greet, 0)
    pl.semaphore_wait(barrier, chips)

    swap = pltpu.make_async_remote_copy(
        src_ref=part_ref.at[1 - core], dst_ref=sib, send_sem=sib_send, recv_sem=sib_recv,
        device_id={"hours": twin}, device_id_type=MESH,
    )
    swap.start()
    swap.wait()
    for q in range(chips):
        columns = slice(q * width, (q + 1) * width)
        outgoing[q] = part_ref[core, :, columns] + sib[:, columns]
    incoming[chip] = outgoing[chip]

    def sending(d):
        goal = lax.rem(chip + d, chips)
        return pltpu.make_async_remote_copy(
            src_ref=outgoing.at[goal], dst_ref=incoming.at[chip],
            send_sem=out_send.at[d - 1], recv_sem=in_recv.at[d - 1],
            device_id={"hours": 2 * goal + core}, device_id_type=MESH,
        )

    def start_send(d, carry):
        sending(d).start()
        return carry

    def wait_send(d, carry):
        sending(d).wait()
        return carry

    lax.fori_loop(1, chips, start_send, 0)
    lax.fori_loop(1, chips, wait_send, 0)
    merged = incoming[0]
    for q in range(1, chips):
        merged = merged + incoming[q]
    total[...] = merged
    vectors = [total[r * each : (r + 1) * each] for r in range(RANK)]
    lane = lax.broadcasted_iota(jnp.int32, (1, 128), 1)
    tile = jnp.zeros((each, 128), F32)
    order = [(i, j) for i in range(RANK) for j in range(i + 1)]
    for index, (i, j) in enumerate(order):
        value = jnp.sum(vectors[i] * vectors[j], axis=1, keepdims=True)
        tile = tile + jnp.where(lane == index, value, 0.0)
    grams[chip, :each] = tile

    def telling(d):
        goal = lax.rem(chip + d, chips)
        return pltpu.make_async_remote_copy(
            src_ref=grams.at[chip], dst_ref=grams.at[chip],
            send_sem=gram_send.at[d - 1], recv_sem=gram_recv.at[d - 1],
            device_id={"hours": 2 * goal + core}, device_id_type=MESH,
        )

    def start_tell(d, carry):
        telling(d).start()
        return carry

    def wait_tell(d, carry):
        telling(d).wait()
        return carry

    lax.fori_loop(1, chips, start_tell, 0)
    lax.fori_loop(1, chips, wait_tell, 0)
    summed = grams[0, :each]
    for q in range(1, chips):
        summed = summed + grams[q, :each]
    small = [[None] * RANK for _ in range(RANK)]
    for index, (i, j) in enumerate(order):
        small[i][j] = summed[:, index : index + 1]
    result = solve(cholesky(small), vectors)
    for r in range(RANK):
        fin[r * each : (r + 1) * each] = result[r] * math.sqrt(lags)
    fin[RANK * each :] = total[RANK * each :]

    last = pltpu.make_async_remote_copy(
        src_ref=fin, dst_ref=theirs, send_sem=fin_send, recv_sem=fin_recv,
        device_id={"hours": twin}, device_id_type=MESH,
    )
    last.start()
    own_half = width // 2

    def mine(x):
        return jnp.where(core == 0, x[:, :own_half], x[:, own_half:])

    out_ref[core] = mine(fin[...])
    last.wait()
    out_ref[1 - core] = mine(theirs[...])


def on_device(table, spectra, masks, pair_rows, start_basis):
    stations, windows, segments, _, freq = spectra.shape
    lags = start_basis.shape[1]
    half = lags // 2
    pairs = pair_rows.shape[0]
    block = windows * segments
    count = pairs * block
    batches = pairs * windows
    each = pairs // 2
    slots = 32
    chips = lax.axis_size("hours") // 2
    width = lags // chips
    whitened = whiten(spectra, masks).transpose(0, 3, 1, 2, 4).reshape(stations, 2, block, freq)
    vmem = pl.BlockSpec(memory_space=pltpu.VMEM)
    hbm = pl.BlockSpec(memory_space=pl.ANY)
    windows_out, part = pl.pallas_call(
        functools.partial(correlate_kernel, stations, segments, windows, pairs, freq, half),
        out_shape=(
            jax.ShapeDtypeStruct((batches, lags), F32),
            jax.ShapeDtypeStruct((2, slots, lags), F32),
        ),
        in_specs=[pl.BlockSpec(memory_space=pltpu.SMEM), hbm, hbm, vmem],
        out_specs=(vmem, vmem),
        scratch_shapes=[
            pltpu.VMEM((3 * stations, 2, block, freq), BF16),
            pltpu.VMEM((2 * count, 2 * freq), BF16),
            pltpu.VMEM((2 * freq, half), BF16),
            pltpu.VMEM((2, 256, half), BF16),
            pltpu.VMEM((2, 256, half), BF16),
            pltpu.VMEM((count, 128), F32),
            pltpu.VMEM((2, batches, 128), F32),
            pltpu.VMEM((batches + 2 * slots, 256), F32),
            pltpu.SemaphoreType.DMA((2,)),
            pltpu.SemaphoreType.DMA((2,)),
            pltpu.SemaphoreType.DMA((2,)),
        ],
        compiler_params=pltpu.CompilerParams(
            collective_id=0, has_side_effects=True, vmem_limit_bytes=40 << 20
        ),
        name="correlate",
    )(pair_rows, whitened, table, start_basis)
    merged = pl.pallas_call(
        functools.partial(merge_kernel, each, lags),
        out_shape=jax.ShapeDtypeStruct((2, slots, width // 2), F32),
        in_specs=[vmem],
        out_specs=vmem,
        scratch_shapes=[
            pltpu.VMEM((slots, lags), F32),
            pltpu.VMEM((chips, slots, width), F32),
            pltpu.VMEM((chips, slots, width), F32),
            pltpu.VMEM((slots, width), F32),
            pltpu.VMEM((chips, 8, 128), F32),
            pltpu.VMEM((slots, width), F32),
            pltpu.VMEM((slots, width), F32),
            pltpu.SemaphoreType.DMA,
            pltpu.SemaphoreType.DMA,
            pltpu.SemaphoreType.DMA((chips - 1,)),
            pltpu.SemaphoreType.DMA((chips - 1,)),
            pltpu.SemaphoreType.DMA((chips - 1,)),
            pltpu.SemaphoreType.DMA((chips - 1,)),
            pltpu.SemaphoreType.DMA,
            pltpu.SemaphoreType.DMA,
        ],
        compiler_params=pltpu.CompilerParams(
            collective_id=1, has_side_effects=True, vmem_limit_bytes=16 << 20
        ),
        name="merge",
    )(part)
    window_stacks = windows_out.reshape(pairs, windows, lags)
    basis = merged[:, : RANK * each].reshape(2, RANK, each, width // 2)
    basis = basis.transpose(0, 2, 1, 3).reshape(pairs, RANK, width // 2)
    stack = merged[:, RANK * each : (RANK + 1) * each].reshape(pairs, width // 2)
    return (window_stacks, stack, basis)


def solution(mesh):
    in_specs = (
        P("pairs", "hours", None, None, None),
        P("pairs", "hours", None),
        P("pairs", None),
        P(),
    )
    out_specs = (P("pairs", "hours", None), P("pairs", "hours"), P("pairs", None, "hours"))

    def whole(spectra, masks, pair_rows, start_basis):
        table = jnp.asarray(half_table(spectra.shape[4], start_basis.shape[1] // 2))
        return jax.shard_map(
            on_device, mesh=mesh, in_specs=(P(), *in_specs), out_specs=out_specs, check_vma=False
        )(table, spectra, masks, pair_rows, start_basis)

    return whole
```

time: 254 us -> 63.3 us (0.25)
  waiting for transfers between devices: 133 us -> 0 us
  Pallas kernels: 0 us -> 53.5 us
  other arithmetic: 46.7 us -> 3.45 us
  matrix products: 36.1 us -> 0 us
  starting transfers between devices: 13.9 us -> 0 us
  between operations: 14.4 us -> 0.77 us
  local copies, waits for them, and re-layouts: 9.85 us -> 5.36 us
    psum x1 -> x0, waiting for transfers between devices: 133 us -> none  [on_device(): merged, stack_whole = lax.psum((merged_terms, stack_terms), 'hours')]
    pallas_call x0 -> x2, Pallas kernels: none -> 53.5 us  [the longest x1 30.6 us: on_device(): pl.pallas_call(functools.partial(correlate_kernel, stations, segments, wi...]
    dot_general x12 -> x0, matrix products: 36.1 us -> none  [the longest x3 10.7 us: power_step(): proj = jnp.einsum('pwrl,pwgl->pwrg', basis, corr, precision=HIGH)]
    another operation x1 -> x0, other arithmetic: 35.8 us -> none
    ppermute x2 -> x0, starting transfers between devices: 13.9 us -> none  [the longest x1 9.5 us: padded(): lax.ppermute(lax.slice_in_dim(block, 0, width, axis=dim), axis, backward)]
    div x4 -> x0, other arithmetic: 6.5 us -> none  [the longest x3 5.83 us: from_gram(): result.append(current / lower[row][row][..., None])]
    slice x21 -> x3, local copies, waits for them, and re-layouts: 2.62 us -> 0.02 us  [the longest x2 0.02 us: on_device(): basis = merged[:, :RANK * each].reshape(2, RANK, each, width // 2)]
  transfers between devices with their start and end apart: 3 -> 0, of which waited for: 1 -> 0; matrix products, arithmetic and copies ran while one was open for 14% -> 0% of each run, Pallas kernels for 0% -> 0%
where the time goes in v1:
time: 63.3 us; the launch traced here: 63.1 us
  Pallas kernels  53.5 us (85%)
  local copies, waits for them, and re-layouts  5.36 us (8%)
  other arithmetic  3.45 us (5%)
  between operations  0.77 us (1%)
    pallas_call x1, Pallas kernels, on_device(): pl.pallas_call(functools.partial(correlate_kernel, stations, segments, wi...  30.6 us
    pallas_call x1, Pallas kernels, on_device(): pl.pallas_call(functools.partial(merge_kernel, each, lags), out_shape=jax...  22.9 us
    reduce_sum x2, other arithmetic, whiten(): power = jnp.mean(banded * banded, axis=(3, 5), keepdims=True)  2.82 us
    unnamed x11, local copies, waits for them, and re-layouts  2.3 us

profile of v1, /device:TPU:1, one launch (start us, length us, event | category | flops | bytes accessed | tf_op | source)
XLA Modules:
  0.0 63.1 jit_solution(8239818919386969463)
XLA Ops:
  0.6 0.0 copy-start.2
  0.6 0.0 copy-start.3
  0.6 2.5 %fusion = f32[8,2,8,1024]{3,2,1,0:T(8,128)S(1)} fusion(bf16[8,2,8,2,1024]{4,3,2,1,0:T(2,128)(2,1)} %param.5), kind=kLoop, calls=%fused_computation.2 | loop fusion | flops 655360 | bytes 1048576 | tf_op jit(solution)/shard_map/reduce_sum | solution.py:34
  3.1 0.0 copy-start.4
  3.1 0.0 copy-start.1
  3.2 0.3 reduce_sum.14
  3.4 0.3 reduce_sum.18
  3.8 0.3 mul.27
  4.1 0.3 mul.28
  4.5 0.0 copy-done.3
  4.5 0.0 copy-done.2
  4.5 0.6 fusion.3
  5.1 0.1 copy.23
  5.2 0.0 copy-done.4
  5.2 0.1 copy.19.rows_ref
  5.3 0.0 copy-done.1
  5.3 0.0 copy-start
  5.3 2.2 %copy-done = bf16[2048,1024]{1,0:T(8,128)(2,1)S(1)} copy-done((bf16[2048,1024]{1,0:T(8,128)(2,1)S(1)}, bf16[2048,1024]{1,0:T(8,128)(2,1)}, u32[]{:S(2)}) %copy-start) | copy-done | bytes 4194328
  7.5 30.6 %correlate.1 = (f32[24,2048]{1,0:T(8,128)S(1)}, f32[2,32,2048]{2,1,0:T(8,128)S(1)}) custom-call(s32[12,2]{1,0:T(8,128)S(1)} %copy.19.rows_ref, bf16[8,2,16,1024]{3,2,1,0:T(8,128)(2,1)S(1)} %bitcast.13, bf16[2048,1024]{1,0:T(8,128)(2,1)S(1)} %copy-done, f32[4,2048]{1,0:T(4,128)S(1)} %copy-done.1), custom_call_target="tpu_custom_call" | custom-call | tf_op jit(solution)/shard_map/correlate/pallas_call | solution.py:384
  38.2 22.9 %merge.1 = f32[2,32,64]{2,1,0:T(8,128)S(1)} custom-call(f32[2,32,2048]{2,1,0:T(8,128)S(1)} %get-tuple-element.6.part_ref), custom_call_target="tpu_custom_call" | custom-call | tf_op jit(solution)/shard_map/merge/pallas_call | solution.py:410
  61.1 0.6 copy.21
  61.7 0.6 reshape.36
  62.3 0.8 %reshape.35 = f32[12,2,2048]{2,1,0:T(2,128)} reshape(f32[24,2048]{1,0:T(8,128)S(1)} %get-tuple-element.5) | data formatting | bytes 393216 | tf_op jit(solution)/shard_map/reshape | solution.py:437
  (5 shorter events, 0.0 us)
Async XLA Ops:
  0.6 3.9 %copy-start.2 = (bf16[8,2,8,2,1024]{4,3,2,1,0:T(2,128)(2,1)S(1)}, bf16[8,2,8,2,1024]{4,3,2,1,0:T(2,128)(2,1)}, u32[]{:S(2)}) copy-start(bf16[8,2,8,2,1024]{4,3,2,1,0:T(2,128)(2,1)} %param.5) | copy-start | bytes 1572868
  0.6 3.8 %copy-start.3 = (s32[8,2,8]{2,1,0:T(2,128)S(1)}, s32[8,2,8]{2,1,0:T(2,128)}, u32[]{:S(2)}) copy-start(s32[8,2,8]{2,1,0:T(2,128)} %param.6) | copy-start | bytes 1540
  3.1 2.1 %copy-start.4 = (s32[12,2]{0,1:T(2,128)S(1)}, s32[12,2]{0,1:T(2,128)}, u32[]{:S(2)}) copy-start(s32[12,2]{0,1:T(2,128)} %param.7) | copy-start | bytes 292
  3.1 2.2 %copy-start.1 = (f32[4,2048]{1,0:T(4,128)S(1)}, f32[4,2048]{1,0:T(4,128)}, u32[]{:S(2)}) copy-start(f32[4,2048]{1,0:T(4,128)} %start_ref.1) | copy-start | bytes 98308
  5.3 2.2 %copy-start = (bf16[2048,1024]{1,0:T(8,128)(2,1)S(1)}, bf16[2048,1024]{1,0:T(8,128)(2,1)}, u32[]{:S(2)}) copy-start(bf16[2048,1024]{1,0:T(8,128)(2,1)} %constant.9.clone.table_ref) | copy-start | bytes 12582916

commit v2 on v1

--- a/solution.py
+++ b/solution.py
@@ -17,11 +17,10 @@
 BF16 = jnp.bfloat16
 
 
-def half_table(freq, half):
-    nfft = 4 * half
+def full_table(freq, lags):
     bins = np.arange(1, freq + 1, dtype=np.int64)[:, None]
-    shifts = np.arange(half, dtype=np.int64)[None, :]
-    phase = np.mod(bins * shifts, nfft).astype(np.float64) * (2.0 * math.pi / nfft)
+    shifts = np.arange(lags, dtype=np.int64)[None, :] - lags // 2
+    phase = np.mod(bins * shifts, 2 * lags).astype(np.float64) * (math.pi / lags)
     scale = freq ** (-0.5)
     table = np.concatenate([np.cos(phase) * scale, -np.sin(phase) * scale], 0)
     return table.astype(np.float32).astype(jnp.bfloat16)
@@ -74,12 +73,23 @@
     return total
 
 
-def correlate_kernel(
+def torus_offsets(chips):
+    side = math.isqrt(chips)
+    side = side if side * side == chips else 1
+    other = chips // side
+    offsets = [(dx, dy) for dx in range(other) for dy in range(side) if dx or dy]
+    return side, other, sorted(
+        offsets, key=lambda o: -(min(o[0], other - o[0]) + min(o[1], side - o[1]))
+    )
+
+
+def station_kernel(
     stations, segments, windows, pairs, freq, half,
     rows_ref, wh_ref, table_ref, start_ref,
-    ws_ref, part_ref,
+    ws_ref, out_ref,
     near, cross, table, vhi, vlo, square, wide, coef,
-    send_sem, recv_sem, own_sem,
+    part, sib, keep, outgoing, incoming, summed_rows, grams, fin, theirs,
+    send_sem, recv_sem, own_sem, out_send, in_recv, gram_send, gram_recv,
 ):
     me, ring = lax.axis_index("pairs"), lax.axis_size("pairs")
     after, before = lax.rem(me + 1, ring), lax.rem(me + ring - 1, ring)
@@ -93,10 +103,21 @@
     own.start()
     fill.start()
 
+    hour = lax.axis_index("hours")
+    chips = lax.axis_size("hours") // 2
+    core, chip = lax.rem(hour, 2), lax.div(hour, 2)
+    twin = {"hours": hour + 1 - 2 * core}
+    side, other_side, offsets = torus_offsets(chips)
+    goals = [
+        side * lax.rem(lax.div(chip, side) + dx, other_side) + lax.rem(lax.rem(chip, side) + dy, side)
+        for dx, dy in offsets
+    ]
     barrier = pltpu.get_barrier_semaphore()
-    for other in (before, after):
-        pl.semaphore_signal(barrier, inc=1, device_id={"pairs": other}, device_id_type=MESH)
-    pl.semaphore_wait(barrier, 2)
+    partners = [{"pairs": before}, {"pairs": after}, twin]
+    partners += [{"hours": 2 * goal + core} for goal in goals]
+    for other in partners:
+        pl.semaphore_signal(barrier, inc=1, device_id=other, device_id_type=MESH)
+    pl.semaphore_wait(barrier, len(partners))
     sends = []
     for index, (other, slot) in enumerate(((after, 0), (before, 2 * stations))):
         copy = pltpu.make_async_remote_copy(
@@ -123,11 +144,6 @@
     for copy in sends:
         copy.wait()
 
-    turn = lax.rem(lax.broadcasted_iota(jnp.int32, (1, freq), 1), 4)
-    swap = lax.rem(turn, 2) == 0
-    sign_re = jnp.where((turn == 0) | (turn == 3), 1.0, -1.0)
-    sign_im = jnp.where(turn >= 2, 1.0, -1.0)
-
     def pair_body(p, carry):
         first, second = rows_ref[p, 0], rows_ref[p, 1]
         relative = lax.rem(lax.div(second, stations) - me + 1 + ring, ring)
@@ -138,30 +154,27 @@
         b = near[at_b].astype(F32)
         re = a[0] * b[0] + a[1] * b[1]
         im = a[1] * b[0] - a[0] * b[1]
-        low, high = pl.ds(pl.multiple_of(p * block, block), block), pl.ds(
-            pl.multiple_of(count + p * block, block), block
-        )
-        cross[high, :freq] = re.astype(BF16)
-        cross[high, freq:] = im.astype(BF16)
-        cross[low, :freq] = (jnp.where(swap, im, re) * sign_re).astype(BF16)
-        cross[low, freq:] = (jnp.where(swap, re, im) * sign_im).astype(BF16)
+        rows = pl.ds(pl.multiple_of(p * block, block), block)
+        cross[rows, :freq] = re.astype(BF16)
+        cross[rows, freq:] = im.astype(BF16)
         return carry
 
-    lax.fori_loop(0, pairs, pair_body, 0)
+    lax.fori_loop(0, pairs, pair_body, 0, unroll=2)
     fill.wait()
     tile = 256
 
-    def lag_body(n, carry):
-        columns = pl.ds(pl.multiple_of(n * tile, tile), tile)
-        y = jnp.dot(cross[...], table[:, columns], preferred_element_type=F32)
-        hi, lo = split(y)
-        vhi[0, :count, columns] = hi[:count]
-        vhi[1, :count, columns] = hi[count:]
-        vlo[0, :count, columns] = lo[:count]
-        vlo[1, :count, columns] = lo[count:]
-        return carry
-
-    lax.fori_loop(0, half // tile, lag_body, 0)
+    for h in range(2):
+
+        def lag_body(n, carry, h=h):
+            columns = pl.ds(pl.multiple_of(n * tile, tile), tile)
+            source = pl.ds(pl.multiple_of(h * half + n * tile, tile), tile)
+            y = jnp.dot(cross[...], table[:, source], preferred_element_type=F32)
+            hi, lo = split(y)
+            vhi[h, :count, columns] = hi
+            vlo[h, :count, columns] = lo
+            return carry
+
+        lax.fori_loop(0, half // tile, lag_body, 0)
 
     gram = None
     for h in range(2):
@@ -254,92 +267,55 @@
             columns = slice(h * half + n * 512, h * half + (n + 1) * 512)
             ws_ref[:, columns] = out[:batches]
             for c in range(2):
-                part_ref[c, :, columns] = out[batches + c * slots : batches + (c + 1) * slots]
-
-
-def merge_kernel(
-    each, lags, part_ref, out_ref, sib, outgoing, incoming, total, grams, fin, theirs,
-    sib_send, sib_recv, out_send, in_recv, gram_send, gram_recv, fin_send, fin_recv,
-):
-    hour = lax.axis_index("hours")
-    chips = lax.axis_size("hours") // 2
-    core, chip = lax.rem(hour, 2), lax.div(hour, 2)
-    twin = hour + 1 - 2 * core
+                part[c, :, columns] = out[batches + c * slots : batches + (c + 1) * slots]
+
+
     width = lags // chips
-
-    barrier = pltpu.get_barrier_semaphore()
-    pl.semaphore_signal(barrier, inc=1, device_id={"hours": twin}, device_id_type=MESH)
-
-    def target(d):
-        return 2 * lax.rem(chip + d, chips) + core
-
-    def greet(d, carry):
-        pl.semaphore_signal(barrier, inc=1, device_id={"hours": target(d)}, device_id_type=MESH)
-        return carry
-
-    lax.fori_loop(1, chips, greet, 0)
-    pl.semaphore_wait(barrier, chips)
-
     swap = pltpu.make_async_remote_copy(
-        src_ref=part_ref.at[1 - core], dst_ref=sib, send_sem=sib_send, recv_sem=sib_recv,
-        device_id={"hours": twin}, device_id_type=MESH,
+        src_ref=part.at[1 - core], dst_ref=sib, send_sem=send_sem.at[2], recv_sem=recv_sem.at[2],
+        device_id=twin, device_id_type=MESH,
     )
     swap.start()
     swap.wait()
     for q in range(chips):
         columns = slice(q * width, (q + 1) * width)
-        outgoing[q] = part_ref[core, :, columns] + sib[:, columns]
-    incoming[chip] = outgoing[chip]
-
-    def sending(d):
-        goal = lax.rem(chip + d, chips)
-        return pltpu.make_async_remote_copy(
-            src_ref=outgoing.at[goal], dst_ref=incoming.at[chip],
-            send_sem=out_send.at[d - 1], recv_sem=in_recv.at[d - 1],
+        keep[q] = part[core, :, columns] + sib[:, columns]
+        outgoing[q] = keep[q].astype(BF16)
+    sends = []
+    for index, goal in enumerate(goals):
+        copy = pltpu.make_async_remote_copy(
+            src_ref=outgoing.at[goal], dst_ref=incoming.at[index],
+            send_sem=out_send.at[index], recv_sem=in_recv.at[index],
             device_id={"hours": 2 * goal + core}, device_id_type=MESH,
         )
-
-    def start_send(d, carry):
-        sending(d).start()
-        return carry
-
-    def wait_send(d, carry):
-        sending(d).wait()
-        return carry
-
-    lax.fori_loop(1, chips, start_send, 0)
-    lax.fori_loop(1, chips, wait_send, 0)
-    merged = incoming[0]
-    for q in range(1, chips):
-        merged = merged + incoming[q]
-    total[...] = merged
-    vectors = [total[r * each : (r + 1) * each] for r in range(RANK)]
+        copy.start()
+        sends.append(copy)
+    merged = keep[chip]
+    for copy in reversed(sends):
+        copy.wait()
+    for index in range(chips - 1):
+        merged = merged + incoming[index].astype(F32)
+    summed_rows[...] = merged
+    vectors = [summed_rows[r * each : (r + 1) * each] for r in range(RANK)]
     lane = lax.broadcasted_iota(jnp.int32, (1, 128), 1)
     tile = jnp.zeros((each, 128), F32)
     order = [(i, j) for i in range(RANK) for j in range(i + 1)]
     for index, (i, j) in enumerate(order):
         value = jnp.sum(vectors[i] * vectors[j], axis=1, keepdims=True)
         tile = tile + jnp.where(lane == index, value, 0.0)
-    grams[chip, :each] = tile
-
-    def telling(d):
-        goal = lax.rem(chip + d, chips)
-        return pltpu.make_async_remote_copy(
-            src_ref=grams.at[chip], dst_ref=grams.at[chip],
-            send_sem=gram_send.at[d - 1], recv_sem=gram_recv.at[d - 1],
+    grams[chips - 1, :each] = tile
+
+    sends = []
+    for index, goal in enumerate(goals):
+        copy = pltpu.make_async_remote_copy(
+            src_ref=grams.at[chips - 1], dst_ref=grams.at[index],
+            send_sem=gram_send.at[index], recv_sem=gram_recv.at[index],
             device_id={"hours": 2 * goal + core}, device_id_type=MESH,
         )
-
-    def start_tell(d, carry):
-        telling(d).start()
-        return carry
-
-    def wait_tell(d, carry):
-        telling(d).wait()
-        return carry
-
-    lax.fori_loop(1, chips, start_tell, 0)
-    lax.fori_loop(1, chips, wait_tell, 0)
+        copy.start()
+        sends.append(copy)
+    for copy in reversed(sends):
+        copy.wait()
     summed = grams[0, :each]
     for q in range(1, chips):
         summed = summed + grams[q, :each]
@@ -349,11 +325,11 @@
     result = solve(cholesky(small), vectors)
     for r in range(RANK):
         fin[r * each : (r + 1) * each] = result[r] * math.sqrt(lags)
-    fin[RANK * each :] = total[RANK * each :]
+    fin[RANK * each :] = summed_rows[RANK * each :]
 
     last = pltpu.make_async_remote_copy(
-        src_ref=fin, dst_ref=theirs, send_sem=fin_send, recv_sem=fin_recv,
-        device_id={"hours": twin}, device_id_type=MESH,
+        src_ref=fin, dst_ref=theirs, send_sem=send_sem.at[3], recv_sem=recv_sem.at[3],
+        device_id=twin, device_id_type=MESH,
     )
     last.start()
     own_half = width // 2
@@ -380,60 +356,50 @@
     width = lags // chips
     whitened = whiten(spectra, masks).transpose(0, 3, 1, 2, 4).reshape(stations, 2, block, freq)
     vmem = pl.BlockSpec(memory_space=pltpu.VMEM)
-    hbm = pl.BlockSpec(memory_space=pl.ANY)
-    windows_out, part = pl.pallas_call(
-        functools.partial(correlate_kernel, stations, segments, windows, pairs, freq, half),
+    windows_out, merged = pl.pallas_call(
+        functools.partial(station_kernel, stations, segments, windows, pairs, freq, half),
         out_shape=(
             jax.ShapeDtypeStruct((batches, lags), F32),
-            jax.ShapeDtypeStruct((2, slots, lags), F32),
+            jax.ShapeDtypeStruct((2, slots, width // 2), F32),
         ),
-        in_specs=[pl.BlockSpec(memory_space=pltpu.SMEM), hbm, hbm, vmem],
+        in_specs=[
+            pl.BlockSpec(memory_space=pltpu.SMEM),
+            pl.BlockSpec(memory_space=pl.ANY),
+            pl.BlockSpec(memory_space=pltpu.HBM),
+            vmem,
+        ],
         out_specs=(vmem, vmem),
         scratch_shapes=[
             pltpu.VMEM((3 * stations, 2, block, freq), BF16),
-            pltpu.VMEM((2 * count, 2 * freq), BF16),
-            pltpu.VMEM((2 * freq, half), BF16),
+            pltpu.VMEM((count, 2 * freq), BF16),
+            pltpu.VMEM((2 * freq, lags), BF16),
             pltpu.VMEM((2, 256, half), BF16),
             pltpu.VMEM((2, 256, half), BF16),
             pltpu.VMEM((count, 128), F32),
             pltpu.VMEM((2, batches, 128), F32),
             pltpu.VMEM((batches + 2 * slots, 256), F32),
-            pltpu.SemaphoreType.DMA((2,)),
-            pltpu.SemaphoreType.DMA((2,)),
-            pltpu.SemaphoreType.DMA((2,)),
-        ],
-        compiler_params=pltpu.CompilerParams(
-            collective_id=0, has_side_effects=True, vmem_limit_bytes=40 << 20
-        ),
-        name="correlate",
-    )(pair_rows, whitened, table, start_basis)
-    merged = pl.pallas_call(
-        functools.partial(merge_kernel, each, lags),
-        out_shape=jax.ShapeDtypeStruct((2, slots, width // 2), F32),
-        in_specs=[vmem],
-        out_specs=vmem,
-        scratch_shapes=[
+            pltpu.VMEM((2, slots, lags), F32),
             pltpu.VMEM((slots, lags), F32),
             pltpu.VMEM((chips, slots, width), F32),
-            pltpu.VMEM((chips, slots, width), F32),
+            pltpu.VMEM((chips, slots, width), BF16),
+            pltpu.VMEM((chips - 1, slots, width), BF16),
             pltpu.VMEM((slots, width), F32),
             pltpu.VMEM((chips, 8, 128), F32),
             pltpu.VMEM((slots, width), F32),
             pltpu.VMEM((slots, width), F32),
-            pltpu.SemaphoreType.DMA,
-            pltpu.SemaphoreType.DMA,
+            pltpu.SemaphoreType.DMA((4,)),
+            pltpu.SemaphoreType.DMA((4,)),
+            pltpu.SemaphoreType.DMA((2,)),
             pltpu.SemaphoreType.DMA((chips - 1,)),
             pltpu.SemaphoreType.DMA((chips - 1,)),
             pltpu.SemaphoreType.DMA((chips - 1,)),
             pltpu.SemaphoreType.DMA((chips - 1,)),
-            pltpu.SemaphoreType.DMA,
-            pltpu.SemaphoreType.DMA,
         ],
         compiler_params=pltpu.CompilerParams(
-            collective_id=1, has_side_effects=True, vmem_limit_bytes=16 << 20
+            collective_id=0, has_side_effects=True, vmem_limit_bytes=48 << 20
         ),
-        name="merge",
-    )(part)
+        name="station_pairs",
+    )(pair_rows, whitened, table, start_basis)
     window_stacks = windows_out.reshape(pairs, windows, lags)
     basis = merged[:, : RANK * each].reshape(2, RANK, each, width // 2)
     basis = basis.transpose(0, 2, 1, 3).reshape(pairs, RANK, width // 2)
@@ -451,7 +417,7 @@
     out_specs = (P("pairs", "hours", None), P("pairs", "hours"), P("pairs", None, "hours"))
 
     def whole(spectra, masks, pair_rows, start_basis):
-        table = jnp.asarray(half_table(spectra.shape[4], start_basis.shape[1] // 2))
+        table = jnp.asarray(full_table(spectra.shape[4], start_basis.shape[1]))
         return jax.shard_map(
             on_device, mesh=mesh, in_specs=(P(), *in_specs), out_specs=out_specs, check_vma=False
         )(table, spectra, masks, pair_rows, start_basis)

time: 63.3 us -> 59.4 us (0.938)
  Pallas kernels: 53.5 us -> 50.1 us
  local copies, waits for them, and re-layouts: 5.36 us -> 3.16 us
  other arithmetic: 3.45 us -> 5.14 us
    pallas_call x2 -> x1, Pallas kernels: 53.5 us -> 50.1 us  [on_device(): pl.pallas_call(functools.partial(station_kernel, stations, segments, wind...]
    unnamed x11 -> x5, local copies, waits for them, and re-layouts: 2.3 us -> 0.1 us
    transpose x1, other arithmetic: 0.6 us -> 1.64 us  [on_device(): whiten(spectra, masks).transpose(0, 3, 1, 2, 4)]
    convert_element_type x1, other arithmetic: 0.01 us -> 0.7 us  [whiten(): masks.astype(F32)[:, :, :, None, None, None]]
where the time goes in v2:
time: 59.4 us; the launch traced here: 59.1 us
  Pallas kernels  50.1 us (84%)
  other arithmetic  5.14 us (9%)
  local copies, waits for them, and re-layouts  3.16 us (5%)
  between operations  0.73 us (1%)
    pallas_call x1, Pallas kernels, on_device(): pl.pallas_call(functools.partial(station_kernel, stations, segments, wind...  50.1 us
    reduce_sum x2, other arithmetic, whiten(): power = jnp.mean(banded * banded, axis=(3, 5), keepdims=True)  2.77 us
    transpose x1, other arithmetic, on_device(): whiten(spectra, masks).transpose(0, 3, 1, 2, 4)  1.64 us

profile of v2, /device:TPU:1, one launch (start us, length us, event | category | flops | bytes accessed | tf_op | source)
XLA Modules:
  0.0 59.1 jit_solution(7855511843011406577)
XLA Ops:
  0.6 0.0 copy-start.1
  0.6 0.0 copy-start
  0.7 2.4 %fusion = f32[8,2,8,1024]{3,2,1,0:T(8,128)S(1)} fusion(bf16[8,2,8,2,1024]{4,3,2,1,0:T(2,128)(2,1)} %param.5), kind=kLoop, calls=%fused_computation.2 | loop fusion | flops 655360 | bytes 1048576 | tf_op jit(solution)/shard_map/reduce_sum | solution.py:33
  3.1 0.3 reduce_sum.14
  3.4 0.3 reduce_sum.18
  3.7 0.3 mul.27
  4.1 0.3 mul.28
  4.4 0.7 %convert_element_type.10 = f32[8,2,8]{2,1,0:T(2,128)S(1)} convert(s32[8,2,8]{2,1,0:T(2,128)} %param.6) | non-fusion elementwise | flops 128 | bytes 1024 | tf_op jit(solution)/shard_map/convert_element_type | solution.py:34
  5.1 1.6 %fusion.3 = bf16[8,2,2,8,1024]{4,1,3,2,0:T(2,128)(2,1)S(1)} fusion(bf16[8,2,8,2,1024]{4,3,2,1,0:T(2,128)(2,1)} %param.5, f32[8,2,8]{2,1,0:T(2,128)S(1)} %convert_element_type.10, f32[8,2,8,1024]{3,2,1,0:T(8,128)S(1)} %mul.28), kind=kLoop, calls=%fused_computation.5 | loop fusion | flops 1048576 | bytes 1573376 | tf_op jit(solution)/shard_map/transpose | solution.py:357
  6.7 0.1 copy.23
  6.9 0.0 copy-done.1
  6.9 0.1 copy.19.rows_ref
  7.0 0.0 copy-done
  7.0 50.1 %station_pairs.1 = (f32[24,2048]{1,0:T(8,128)S(1)}, f32[2,32,64]{2,1,0:T(8,128)S(1)}) custom-call(s32[12,2]{1,0:T(8,128)S(1)} %copy.19.rows_ref, bf16[8,2,16,1024]{3,2,1,0:T(8,128)(2,1)S(1)} %bitcast.13, bf16[2048,2048]{1,0:T(8,128)(2,1)} %constant.9.clone.table_ref, f32[4,2048]{1,0:T(4,128)S(1)} %copy-done), custom_call_target="tpu_custom_call" | custom-call | tf_op jit(solution)/shard_map/station_pairs/pallas_call | solution.py:359
  57.1 0.6 %copy.21 = f32[2,6,4,64]{3,2,1,0:T(4,128)} copy(f32[2,6,4,64]{3,0,1,2:T(2,128)S(1)} %bitcast.14) | data formatting | bytes 24576 | tf_op jit(solution)/shard_map/transpose | solution.py:405
  57.7 0.6 %reshape.36 = f32[12,64]{1,0:T(8,128)} reshape(f32[2,6,64]{2,1,0:T(8,128)S(1)} %slice.6) | data formatting | bytes 6144 | tf_op jit(solution)/shard_map/reshape | solution.py:406
  58.3 0.8 %reshape.35 = f32[12,2,2048]{2,1,0:T(2,128)} reshape(f32[24,2048]{1,0:T(8,128)S(1)} %get-tuple-element.5) | data formatting | bytes 393216 | tf_op jit(solution)/shard_map/reshape | solution.py:403
  (4 shorter events, 0.0 us)
Async XLA Ops:
  0.6 6.2 %copy-start.1 = (s32[12,2]{0,1:T(2,128)S(1)}, s32[12,2]{0,1:T(2,128)}, u32[]{:S(2)}) copy-start(s32[12,2]{0,1:T(2,128)} %param.7) | copy-start | bytes 292
  0.6 6.3 %copy-start = (f32[4,2048]{1,0:T(4,128)S(1)}, f32[4,2048]{1,0:T(4,128)}, u32[]{:S(2)}) copy-start(f32[4,2048]{1,0:T(4,128)} %start_ref.1) | copy-start | bytes 98308

commit v3 on v2

--- a/solution.py
+++ b/solution.py
@@ -26,13 +26,18 @@
     return table.astype(np.float32).astype(jnp.bfloat16)
 
 
-def whiten(spectra, masks):
-    values = spectra.astype(F32)
-    shape = values.shape
-    banded = values.reshape(shape[:-1] + (shape[-1] // BAND, BAND))
-    power = jnp.mean(banded * banded, axis=(3, 5), keepdims=True)
-    scaled = banded * lax.rsqrt(power + 1e-06) * masks.astype(F32)[:, :, :, None, None, None]
-    return scaled.reshape(shape).astype(BF16)
+def whiten(x, mask, ones):
+    rows, freq = x.shape[1:]
+    square = x[0] * x[0] + x[1] * x[1]
+    tiles = freq // 128
+    stacked = jnp.concatenate([square[:, t * 128 : (t + 1) * 128] for t in range(tiles)], 0)
+    hi, lo = split(stacked)
+    power = jnp.dot(hi, ones, preferred_element_type=F32) + jnp.dot(
+        lo, ones, preferred_element_type=F32
+    )
+    scale = lax.rsqrt(power * (0.5 / BAND) + 1e-06)
+    scale = jnp.concatenate([scale[t * rows : (t + 1) * rows] for t in range(tiles)], 1) * mask
+    return (x[0] * scale).astype(BF16), (x[1] * scale).astype(BF16)
 
 
 def nt(a, b):
@@ -85,11 +90,11 @@
 
 def station_kernel(
     stations, segments, windows, pairs, freq, half,
-    rows_ref, wh_ref, table_ref, start_ref,
+    rows_ref, masks_ref, raw_ref, table_ref, start_ref,
     ws_ref, out_ref,
-    near, cross, table, vhi, vlo, square, wide, coef,
+    raw, mine, packed, wants, asked, near, cross, table, vhi, vlo, square, wide, coef,
     part, sib, keep, outgoing, incoming, summed_rows, grams, fin, theirs,
-    send_sem, recv_sem, own_sem, out_send, in_recv, gram_send, gram_recv,
+    list_send, list_recv, halo_send, halo_recv, send_sem, recv_sem, own_sem, out_send, in_recv, gram_send, gram_recv,
 ):
     me, ring = lax.axis_index("pairs"), lax.axis_size("pairs")
     after, before = lax.rem(me + 1, ring), lax.rem(me + ring - 1, ring)
@@ -98,7 +103,8 @@
     batches = pairs * windows
     lags = 2 * half
     slots = coef.shape[0] // 2 - batches // 2
-    own = pltpu.make_async_copy(wh_ref, near.at[pl.ds(stations, stations)], own_sem.at[0])
+    some = stations // 2
+    own = pltpu.make_async_copy(raw_ref, raw, own_sem.at[0])
     fill = pltpu.make_async_copy(table_ref, table, own_sem.at[1])
     own.start()
     fill.start()
@@ -117,19 +123,77 @@
     partners += [{"hours": 2 * goal + core} for goal in goals]
     for other in partners:
         pl.semaphore_signal(barrier, inc=1, device_id=other, device_id_type=MESH)
+
+    keys = []
+    for p in range(pairs):
+        second = rows_ref[p, 1]
+        relative = lax.rem(lax.div(second, stations) - me + 1 + ring, ring)
+        keys.append(relative * stations + lax.rem(second, stations))
+    place = []
+    for side in range(2):
+        taken, slots_of = 0, []
+        picks = [0] * some
+        for j in range(stations):
+            found = keys[0] == 2 * side * stations + j
+            for key in keys[1:]:
+                found = found | (key == 2 * side * stations + j)
+            used = found.astype(jnp.int32)
+            slots_of.append(taken)
+            for t in range(some):
+                picks[t] = picks[t] + jnp.where(found & (taken == t), j, 0)
+            taken = taken + used
+        place.append(slots_of)
+        for t in range(some):
+            wants[side, t] = picks[t]
     pl.semaphore_wait(barrier, len(partners))
-    sends = []
-    for index, (other, slot) in enumerate(((after, 0), (before, 2 * stations))):
+    asks = []
+    for side, other in ((0, before), (1, after)):
         copy = pltpu.make_async_remote_copy(
-            src_ref=wh_ref,
-            dst_ref=near.at[pl.ds(slot, stations)],
-            send_sem=send_sem.at[index],
-            recv_sem=recv_sem.at[index],
-            device_id={"pairs": other},
-            device_id_type=MESH,
+            src_ref=wants.at[side], dst_ref=asked.at[1 - side],
+            send_sem=list_send.at[side], recv_sem=list_recv.at[1 - side],
+            device_id={"pairs": other}, device_id_type=MESH,
         )
         copy.start()
-        sends.append(copy)
+        asks.append(copy)
+
+    own.wait()
+    ones = jnp.where(
+        lax.div(lax.broadcasted_iota(jnp.int32, (128, 128), 0), BAND)
+        == lax.div(lax.broadcasted_iota(jnp.int32, (128, 128), 1), BAND),
+        1.0, 0.0,
+    ).astype(BF16)
+    diagonal = lax.rem(
+        lax.broadcasted_iota(jnp.int32, (block, segments), 0), segments
+    ) == lax.broadcasted_iota(jnp.int32, (block, segments), 1)
+
+    def station_body(s, carry):
+        flags = masks_ref[s].astype(F32)
+        lines = jnp.concatenate(
+            [jnp.broadcast_to(flags[w : w + 1], (segments, segments)) for w in range(windows)], 0
+        )
+        mask = jnp.sum(jnp.where(diagonal, lines, 0.0), axis=1, keepdims=True)
+        x = jnp.swapaxes(raw[s].astype(F32), 0, 1)
+        re, im = whiten(x, mask, ones)
+        mine[s, 0], mine[s, 1] = re, im
+        near[some + s, 0], near[some + s, 1] = re, im
+        return carry
+
+    lax.fori_loop(0, stations, station_body, 0, unroll=2)
+    sends = []
+    for side, other in ((1, after), (0, before)):
+        asks[1 - side].wait_recv()
+        slot = 0 if side == 1 else some + stations
+        for t in range(some):
+            packed[side, t] = mine[jnp.clip(asked[side, t], 0, stations - 1)]
+            copy = pltpu.make_async_remote_copy(
+                src_ref=packed.at[side, t], dst_ref=near.at[slot + t],
+                send_sem=halo_send.at[side, t], recv_sem=halo_recv.at[side, t],
+                device_id={"pairs": other}, device_id_type=MESH,
+            )
+            copy.start()
+            sends.append(copy)
+    for copy in asks:
+        copy.wait_send()
 
     coef[...] = jnp.zeros_like(coef)
     extra = vhi.shape[1] - count
@@ -140,16 +204,20 @@
         hi, lo = split(rows)
         vhi[h, count:, :] = hi
         vlo[h, count:, :] = lo
-    own.wait()
     for copy in sends:
         copy.wait()
 
     def pair_body(p, carry):
         first, second = rows_ref[p, 0], rows_ref[p, 1]
         relative = lax.rem(lax.div(second, stations) - me + 1 + ring, ring)
-        at_a = stations + lax.rem(first, stations)
-        relative = jnp.minimum(relative, 2)
-        at_b = relative * stations + lax.rem(second, stations)
+        local = lax.rem(second, stations)
+        low, high = place[0][0], some + stations + place[1][0]
+        for j in range(1, stations):
+            low = jnp.where(local == j, place[0][j], low)
+            high = jnp.where(local == j, some + stations + place[1][j], high)
+        at_a = some + lax.rem(first, stations)
+        at_b = jnp.where(relative == 0, low, jnp.where(relative == 1, some + local, high))
+        at_b = jnp.clip(at_b, 0, 2 * stations - 1)
         a = near[at_a].astype(F32)
         b = near[at_b].astype(F32)
         re = a[0] * b[0] + a[1] * b[1]
@@ -334,12 +402,12 @@
     last.start()
     own_half = width // 2
 
-    def mine(x):
+    def halved(x):
         return jnp.where(core == 0, x[:, :own_half], x[:, own_half:])
 
-    out_ref[core] = mine(fin[...])
+    out_ref[core] = halved(fin[...])
     last.wait()
-    out_ref[1 - core] = mine(theirs[...])
+    out_ref[1 - core] = halved(theirs[...])
 
 
 def on_device(table, spectra, masks, pair_rows, start_basis):
@@ -354,7 +422,7 @@
     slots = 32
     chips = lax.axis_size("hours") // 2
     width = lags // chips
-    whitened = whiten(spectra, masks).transpose(0, 3, 1, 2, 4).reshape(stations, 2, block, freq)
+    raw = spectra.reshape(stations, block, 2, freq)
     vmem = pl.BlockSpec(memory_space=pltpu.VMEM)
     windows_out, merged = pl.pallas_call(
         functools.partial(station_kernel, stations, segments, windows, pairs, freq, half),
@@ -364,13 +432,19 @@
         ),
         in_specs=[
             pl.BlockSpec(memory_space=pltpu.SMEM),
-            pl.BlockSpec(memory_space=pl.ANY),
+            vmem,
+            pl.BlockSpec(memory_space=pltpu.HBM),
             pl.BlockSpec(memory_space=pltpu.HBM),
             vmem,
         ],
         out_specs=(vmem, vmem),
         scratch_shapes=[
-            pltpu.VMEM((3 * stations, 2, block, freq), BF16),
+            pltpu.VMEM((stations, block, 2, freq), BF16),
+            pltpu.VMEM((stations, 2, block, freq), BF16),
+            pltpu.VMEM((2, stations // 2, 2, block, freq), BF16),
+            pltpu.SMEM((2, stations // 2), jnp.int32),
+            pltpu.SMEM((2, stations // 2), jnp.int32),
+            pltpu.VMEM((2 * stations, 2, block, freq), BF16),
             pltpu.VMEM((count, 2 * freq), BF16),
             pltpu.VMEM((2 * freq, lags), BF16),
             pltpu.VMEM((2, 256, half), BF16),
@@ -387,6 +461,10 @@
             pltpu.VMEM((chips, 8, 128), F32),
             pltpu.VMEM((slots, width), F32),
             pltpu.VMEM((slots, width), F32),
+            pltpu.SemaphoreType.DMA((2,)),
+            pltpu.SemaphoreType.DMA((2,)),
+            pltpu.SemaphoreType.DMA((2, stations // 2)),
+            pltpu.SemaphoreType.DMA((2, stations // 2)),
             pltpu.SemaphoreType.DMA((4,)),
             pltpu.SemaphoreType.DMA((4,)),
             pltpu.SemaphoreType.DMA((2,)),
@@ -399,7 +477,7 @@
             collective_id=0, has_side_effects=True, vmem_limit_bytes=48 << 20
         ),
         name="station_pairs",
-    )(pair_rows, whitened, table, start_basis)
+    )(pair_rows, masks, raw, table, start_basis)
     window_stacks = windows_out.reshape(pairs, windows, lags)
     basis = merged[:, : RANK * each].reshape(2, RANK, each, width // 2)
     basis = basis.transpose(0, 2, 1, 3).reshape(pairs, RANK, width // 2)

time: 59.4 us -> 52.2 us (0.88)
  other arithmetic: 5.14 us -> 0 us
  Pallas kernels: 50.1 us -> 45.9 us
  local copies, waits for them, and re-layouts: 3.16 us -> 5.28 us
    pallas_call x1, Pallas kernels: 50.1 us -> 45.9 us  [on_device(): pl.pallas_call(functools.partial(station_kernel, stations, segments, wind...]
    unnamed x5 -> x7, local copies, waits for them, and re-layouts: 0.1 us -> 3.26 us
    reduce_sum x2 -> x0, other arithmetic: 2.77 us -> none  [whiten(): power = jnp.mean(banded * banded, axis=(3, 5), keepdims=True)]
    transpose x1 -> x0, other arithmetic: 1.64 us -> none  [on_device(): whiten(spectra, masks).transpose(0, 3, 1, 2, 4)]
    convert_element_type x1 -> x0, other arithmetic: 0.7 us -> none  [whiten(): masks.astype(F32)[:, :, :, None, None, None]]
    mul x2 -> x0, local copies, waits for them, and re-layouts: 0.65 us -> none  [whiten(): banded * lax.rsqrt(power + 1e-06)]
where the time goes in v3:
time: 52.2 us; the launch traced here: 51.9 us
  Pallas kernels  45.9 us (88%)
  local copies, waits for them, and re-layouts  5.28 us (10%)
  between operations  0.65 us (1%)
    pallas_call x1, Pallas kernels, on_device(): pl.pallas_call(functools.partial(station_kernel, stations, segments, wind...  45.9 us
    unnamed x7, local copies, waits for them, and re-layouts  3.26 us

profile of v3, /device:TPU:1, one launch (start us, length us, event | category | flops | bytes accessed | tf_op | source)
XLA Modules:
  0.0 51.9 jit_solution(16699503157605783380)
XLA Ops:
  0.6 0.8 %copy.12.rows_ref = s32[12,2]{1,0:T(8,128)S(1)} copy(s32[12,2]{0,1:T(2,128)} %param.7) | data formatting | bytes 192 | tf_op args[2]
  1.4 0.0 copy-start
  1.4 1.0 %copy-done = bf16[8,2,8,2,1024]{4,3,2,1,0:T(2,128)(2,1)S(1)} copy-done((bf16[8,2,8,2,1024]{4,3,2,1,0:T(2,128)(2,1)S(1)}, bf16[8,2,8,2,1024]{4,3,2,1,0:T(2,128)(2,1)}, u32[]{:S(2)}) %copy-start) | copy-done | bytes 524312
  2.4 0.0 copy-start.1
  2.4 0.8 %copy-done.1 = f32[4,2048]{1,0:T(4,128)S(1)} copy-done((f32[4,2048]{1,0:T(4,128)S(1)}, f32[4,2048]{1,0:T(4,128)}, u32[]{:S(2)}) %copy-start.1) | copy-done | bytes 32792
  3.2 0.0 copy-start.2
  3.2 0.7 %copy-done.2 = s32[8,2,8]{2,1,0:T(2,128)S(1)} copy-done((s32[8,2,8]{2,1,0:T(2,128)S(1)}, s32[8,2,8]{2,1,0:T(2,128)}, u32[]{:S(2)}) %copy-start.2) | copy-done | bytes 536
  3.9 45.9 %station_pairs.1 = (f32[24,2048]{1,0:T(8,128)S(1)}, f32[2,32,64]{2,1,0:T(8,128)S(1)}) custom-call(s32[12,2]{1,0:T(8,128)S(1)} %copy.12.rows_ref, s32[8,2,8]{2,1,0:T(2,128)S(1)} %copy-done.2, bf16[8,16,2,1024]{3,2,1,0:T(2,128)(2,1)S(1)} %bitcast.5, bf16[2048,2048]{1,0:T(8,128)(2,1)} %constant.2.clone.table_ref, f32[4,2048]{1,0:T(4,128)S(1)} %copy-done.1), custom_call_target="tpu_custom_call" | custom-call | tf_op jit(solution)/shard_map/station_pairs/pallas_call | solution.py:427
  49.8 0.8 %reshape.22 = f32[12,2,2048]{2,1,0:T(2,128)} reshape(f32[24,2048]{1,0:T(8,128)S(1)} %get-tuple-element.5) | data formatting | bytes 393216 | tf_op jit(solution)/shard_map/reshape | solution.py:481
  50.6 0.6 %copy.14 = f32[2,6,4,64]{3,2,1,0:T(4,128)} copy(f32[2,6,4,64]{3,0,1,2:T(2,128)S(1)} %bitcast.6) | data formatting | bytes 24576 | tf_op jit(solution)/shard_map/transpose | solution.py:483
  51.3 0.6 %reshape.23 = f32[12,64]{1,0:T(8,128)} reshape(f32[2,6,64]{2,1,0:T(8,128)S(1)} %slice.6) | data formatting | bytes 6144 | tf_op jit(solution)/shard_map/reshape | solution.py:484
  (3 shorter events, 0.0 us)
Async XLA Ops:
  1.4 1.0 %copy-start = (bf16[8,2,8,2,1024]{4,3,2,1,0:T(2,128)(2,1)S(1)}, bf16[8,2,8,2,1024]{4,3,2,1,0:T(2,128)(2,1)}, u32[]{:S(2)}) copy-start(bf16[8,2,8,2,1024]{4,3,2,1,0:T(2,128)(2,1)} %param.5) | copy-start | bytes 1572868
  2.4 0.8 %copy-start.1 = (f32[4,2048]{1,0:T(4,128)S(1)}, f32[4,2048]{1,0:T(4,128)}, u32[]{:S(2)}) copy-start(f32[4,2048]{1,0:T(4,128)} %start_ref.1) | copy-start | bytes 98308
  3.2 0.7 %copy-start.2 = (s32[8,2,8]{2,1,0:T(2,128)S(1)}, s32[8,2,8]{2,1,0:T(2,128)}, u32[]{:S(2)}) copy-start(s32[8,2,8]{2,1,0:T(2,128)} %masks_ref.1) | copy-start | bytes 1540

commit v4 on v3

--- a/solution.py
+++ b/solution.py
@@ -90,9 +90,9 @@
 
 def station_kernel(
     stations, segments, windows, pairs, freq, half,
-    rows_ref, masks_ref, raw_ref, table_ref, start_ref,
+    rows_hbm, masks_hbm, raw_ref, table_ref, start_hbm,
     ws_ref, out_ref,
-    raw, mine, packed, wants, asked, near, cross, table, vhi, vlo, square, wide, coef,
+    rows_ref, masks_ref, start_ref, raw, mine, packed, wants, asked, near, cross, table, vhi, vlo, square, wide, coef,
     part, sib, keep, outgoing, incoming, summed_rows, grams, fin, theirs,
     list_send, list_recv, halo_send, halo_recv, send_sem, recv_sem, own_sem, out_send, in_recv, gram_send, gram_recv,
 ):
@@ -106,6 +106,14 @@
     some = stations // 2
     own = pltpu.make_async_copy(raw_ref, raw, own_sem.at[0])
     fill = pltpu.make_async_copy(table_ref, table, own_sem.at[1])
+    gathers = [
+        pltpu.make_async_copy(source, target, own_sem.at[2 + index])
+        for index, (source, target) in enumerate(
+            ((rows_hbm, rows_ref), (masks_hbm, masks_ref), (start_hbm, start_ref))
+        )
+    ]
+    for copy in gathers:
+        copy.start()
     own.start()
     fill.start()
 
@@ -124,9 +132,10 @@
     for other in partners:
         pl.semaphore_signal(barrier, inc=1, device_id=other, device_id_type=MESH)
 
+    gathers[0].wait()
     keys = []
     for p in range(pairs):
-        second = rows_ref[p, 1]
+        second = rows_ref[1, p]
         relative = lax.rem(lax.div(second, stations) - me + 1 + ring, ring)
         keys.append(relative * stations + lax.rem(second, stations))
     place = []
@@ -157,6 +166,8 @@
         asks.append(copy)
 
     own.wait()
+    for copy in gathers[1:]:
+        copy.wait()
     ones = jnp.where(
         lax.div(lax.broadcasted_iota(jnp.int32, (128, 128), 0), BAND)
         == lax.div(lax.broadcasted_iota(jnp.int32, (128, 128), 1), BAND),
@@ -208,7 +219,7 @@
         copy.wait()
 
     def pair_body(p, carry):
-        first, second = rows_ref[p, 0], rows_ref[p, 1]
+        first, second = rows_ref[0, p], rows_ref[1, p]
         relative = lax.rem(lax.div(second, stations) - me + 1 + ring, ring)
         local = lax.rem(second, stations)
         low, high = place[0][0], some + stations + place[1][0]
@@ -410,6 +421,20 @@
     out_ref[1 - core] = halved(theirs[...])
 
 
+def finish_kernel(pairs, windows, windows_ref, merged_ref, ws_ref, stack_ref, basis_ref):
+    each = pairs // 2
+    for p in range(pairs):
+        ws_ref[p] = windows_ref[windows * p : windows * (p + 1)]
+    rows = merged_ref[...]
+    stack_ref[...] = jnp.concatenate(
+        [rows[c, RANK * each : (RANK + 1) * each] for c in range(2)], 0
+    )
+    for p in range(pairs):
+        c, q = divmod(p, each)
+        for r in range(RANK):
+            basis_ref[p, r : r + 1] = rows[c, r * each + q : r * each + q + 1]
+
+
 def on_device(table, spectra, masks, pair_rows, start_basis):
     stations, windows, segments, _, freq = spectra.shape
     lags = start_basis.shape[1]
@@ -427,18 +452,18 @@
     windows_out, merged = pl.pallas_call(
         functools.partial(station_kernel, stations, segments, windows, pairs, freq, half),
         out_shape=(
-            jax.ShapeDtypeStruct((batches, lags), F32),
-            jax.ShapeDtypeStruct((2, slots, width // 2), F32),
+            pltpu.VMEM((batches, lags), F32),
+            pltpu.VMEM((2, slots, width // 2), F32),
         ),
         in_specs=[
-            pl.BlockSpec(memory_space=pltpu.SMEM),
-            vmem,
             pl.BlockSpec(memory_space=pltpu.HBM),
-            pl.BlockSpec(memory_space=pltpu.HBM),
-            vmem,
-        ],
+        ]
+        * 5,
         out_specs=(vmem, vmem),
         scratch_shapes=[
+            pltpu.SMEM((2, pairs), jnp.int32),
+            pltpu.VMEM((stations, windows, segments), jnp.int32),
+            pltpu.VMEM((RANK, lags), F32),
             pltpu.VMEM((stations, block, 2, freq), BF16),
             pltpu.VMEM((stations, 2, block, freq), BF16),
             pltpu.VMEM((2, stations // 2, 2, block, freq), BF16),
@@ -467,22 +492,29 @@
             pltpu.SemaphoreType.DMA((2, stations // 2)),
             pltpu.SemaphoreType.DMA((4,)),
             pltpu.SemaphoreType.DMA((4,)),
-            pltpu.SemaphoreType.DMA((2,)),
+            pltpu.SemaphoreType.DMA((5,)),
             pltpu.SemaphoreType.DMA((chips - 1,)),
             pltpu.SemaphoreType.DMA((chips - 1,)),
             pltpu.SemaphoreType.DMA((chips - 1,)),
             pltpu.SemaphoreType.DMA((chips - 1,)),
         ],
         compiler_params=pltpu.CompilerParams(
-            collective_id=0, has_side_effects=True, vmem_limit_bytes=48 << 20
+            collective_id=0, has_side_effects=True, vmem_limit_bytes=60 << 20
         ),
         name="station_pairs",
-    )(pair_rows, masks, raw, table, start_basis)
-    window_stacks = windows_out.reshape(pairs, windows, lags)
-    basis = merged[:, : RANK * each].reshape(2, RANK, each, width // 2)
-    basis = basis.transpose(0, 2, 1, 3).reshape(pairs, RANK, width // 2)
-    stack = merged[:, RANK * each : (RANK + 1) * each].reshape(pairs, width // 2)
-    return (window_stacks, stack, basis)
+    )(pair_rows.T, masks, raw, table, start_basis)
+    return pl.pallas_call(
+        functools.partial(finish_kernel, pairs, windows),
+        out_shape=(
+            jax.ShapeDtypeStruct((pairs, windows, lags), F32),
+            jax.ShapeDtypeStruct((pairs, width // 2), F32),
+            jax.ShapeDtypeStruct((pairs, RANK, width // 2), F32),
+        ),
+        in_specs=[vmem, vmem],
+        out_specs=(vmem, vmem, vmem),
+        compiler_params=pltpu.CompilerParams(vmem_limit_bytes=4 << 20),
+        name="outputs",
+    )(windows_out, merged)
 
 
 def solution(mesh):

time: 52.2 us -> 46.7 us (0.89)
  local copies, waits for them, and re-layouts: 5.28 us -> 0 us
    unnamed x7 -> x0, local copies, waits for them, and re-layouts: 3.26 us -> none
    reshape x2 -> x0, local copies, waits for them, and re-layouts: 1.38 us -> none  [the longest x1 0.79 us: on_device(): window_stacks = windows_out.reshape(pairs, windows, lags)]
    pallas_call x1, Pallas kernels: 45.9 us -> 45.2 us  [on_device(): pl.pallas_call(functools.partial(station_kernel, stations, segments, wind...]
    pallas_call x0 -> x1, Pallas kernels: none -> 0.74 us  [on_device(): pl.pallas_call(functools.partial(finish_kernel, pairs, windows), out_shap...]
    transpose x1 -> x0, local copies, waits for them, and re-layouts: 0.62 us -> none  [on_device(): basis = basis.transpose(0, 2, 1, 3).reshape(pairs, RANK, width // 2)]
where the time goes in v4:
time: 46.7 us; the launch traced here: 46.5 us
  Pallas kernels  45.9 us (98%)
  between operations  0.64 us (1%)
    pallas_call x1, Pallas kernels, on_device(): pl.pallas_call(functools.partial(station_kernel, stations, segments, wind...  45.2 us

profile of v4, /device:TPU:1, one launch (start us, length us, event | category | flops | bytes accessed | tf_op | source)
XLA Modules:
  0.0 46.5 jit_solution(9896464515404336423)
XLA Ops:
  0.6 45.2 %station_pairs.1 = (f32[24,2048]{1,0:T(8,128)S(1)}, f32[2,32,64]{2,1,0:T(8,128)S(1)}) custom-call(s32[2,12]{1,0:T(2,128)} %bitcast.3, s32[8,2,8]{2,1,0:T(2,128)} %masks_hbm.1, bf16[8,16,2,1024]{3,2,1,0:T(2,128)(2,1)} %bitcast.2, bf16[2048,2048]{1,0:T(8,128)(2,1)} %constant.2.clone.table_ref, f32[4,2048]{1,0:T(4,128)} %start_hbm.1), custom_call_target="tpu_custom_call" | custom-call | tf_op jit(solution)/shard_map/station_pairs/pallas_call | solution.py:452
  45.8 0.7 %outputs.1 = (f32[12,2,2048]{2,1,0:T(2,128)}, f32[12,64]{1,0:T(8,128)}, f32[12,4,64]{2,1,0:T(4,128)}) custom-call(f32[24,2048]{1,0:T(8,128)S(1)} %get-tuple-element.5.windows_ref, f32[2,32,64]{2,1,0:T(8,128)S(1)} %get-tuple-element.6.merged_ref), custom_call_target="tpu_custom_call" | custom-call | tf_op jit(solution)/shard_map/outputs/pallas_call | solution.py:506

commit v5 on v4

--- a/solution.py
+++ b/solution.py
@@ -17,10 +17,10 @@
 BF16 = jnp.bfloat16
 
 
-def full_table(freq, lags):
+def half_table(freq, half):
     bins = np.arange(1, freq + 1, dtype=np.int64)[:, None]
-    shifts = np.arange(lags, dtype=np.int64)[None, :] - lags // 2
-    phase = np.mod(bins * shifts, 2 * lags).astype(np.float64) * (math.pi / lags)
+    shifts = np.arange(half, dtype=np.int64)[None, :]
+    phase = np.mod(bins * shifts, 4 * half).astype(np.float64) * (math.pi / (2 * half))
     scale = freq ** (-0.5)
     table = np.concatenate([np.cos(phase) * scale, -np.sin(phase) * scale], 0)
     return table.astype(np.float32).astype(jnp.bfloat16)
@@ -92,9 +92,11 @@
     stations, segments, windows, pairs, freq, half,
     rows_hbm, masks_hbm, raw_ref, table_ref, start_hbm,
     ws_ref, out_ref,
-    rows_ref, masks_ref, start_ref, raw, mine, packed, wants, asked, near, cross, table, vhi, vlo, square, wide, coef,
-    part, sib, keep, outgoing, incoming, summed_rows, grams, fin, theirs,
-    list_send, list_recv, halo_send, halo_recv, send_sem, recv_sem, own_sem, out_send, in_recv, gram_send, gram_recv,
+    rows_ref, masks_ref, start_ref, raw, mine, packed, wants, asked, places, near,
+    cross, table, held_rows, square, wide, coef,
+    part, sib, outgoing, incoming, summed_rows, grams, fin, theirs,
+    list_send, list_recv, halo_send, halo_recv, send_sem, recv_sem, own_sem, fill_sem,
+    out_send, in_recv, gram_send, gram_recv,
 ):
     me, ring = lax.axis_index("pairs"), lax.axis_size("pairs")
     after, before = lax.rem(me + 1, ring), lax.rem(me + ring - 1, ring)
@@ -105,7 +107,14 @@
     slots = coef.shape[0] // 2 - batches // 2
     some = stations // 2
     own = pltpu.make_async_copy(raw_ref, raw, own_sem.at[0])
-    fill = pltpu.make_async_copy(table_ref, table, own_sem.at[1])
+    cuts = 4
+    band = 2 * freq // cuts
+    fills = [
+        pltpu.make_async_copy(
+            table_ref.at[pl.ds(i * band, band)], table.at[pl.ds(i * band, band)], fill_sem.at[i]
+        )
+        for i in range(cuts)
+    ]
     gathers = [
         pltpu.make_async_copy(source, target, own_sem.at[2 + index])
         for index, (source, target) in enumerate(
@@ -115,15 +124,17 @@
     for copy in gathers:
         copy.start()
     own.start()
-    fill.start()
+    for copy in fills:
+        copy.start()
 
     hour = lax.axis_index("hours")
     chips = lax.axis_size("hours") // 2
     core, chip = lax.rem(hour, 2), lax.div(hour, 2)
     twin = {"hours": hour + 1 - 2 * core}
-    side, other_side, offsets = torus_offsets(chips)
+    across, other_side, offsets = torus_offsets(chips)
     goals = [
-        side * lax.rem(lax.div(chip, side) + dx, other_side) + lax.rem(lax.rem(chip, side) + dy, side)
+        across * lax.rem(lax.div(chip, across) + dx, other_side)
+        + lax.rem(lax.rem(chip, across) + dy, across)
         for dx, dy in offsets
     ]
     barrier = pltpu.get_barrier_semaphore()
@@ -207,59 +218,58 @@
         copy.wait_send()
 
     coef[...] = jnp.zeros_like(coef)
-    extra = vhi.shape[1] - count
-    for h in range(2):
-        rows = jnp.concatenate(
-            [start_ref[:, h * half : (h + 1) * half], jnp.zeros((extra - RANK, half), F32)], 0
-        )
-        hi, lo = split(rows)
-        vhi[h, count:, :] = hi
-        vlo[h, count:, :] = lo
-    for copy in sends:
-        copy.wait()
-
-    def pair_body(p, carry):
-        first, second = rows_ref[0, p], rows_ref[1, p]
-        relative = lax.rem(lax.div(second, stations) - me + 1 + ring, ring)
-        local = lax.rem(second, stations)
+    extra = held_rows.shape[0] - count
+    held_rows[count:, :] = jnp.concatenate(
+        [start_ref[...], jnp.zeros((extra - RANK, lags), F32)], 0
+    ).astype(BF16)
+    for p in range(pairs):
+        local = lax.rem(rows_ref[1, p], stations)
+        relative = lax.div(keys[p], stations)
         low, high = place[0][0], some + stations + place[1][0]
         for j in range(1, stations):
             low = jnp.where(local == j, place[0][j], low)
             high = jnp.where(local == j, some + stations + place[1][j], high)
-        at_a = some + lax.rem(first, stations)
         at_b = jnp.where(relative == 0, low, jnp.where(relative == 1, some + local, high))
-        at_b = jnp.clip(at_b, 0, 2 * stations - 1)
-        a = near[at_a].astype(F32)
-        b = near[at_b].astype(F32)
+        places[0, p] = some + lax.rem(rows_ref[0, p], stations)
+        places[1, p] = jnp.clip(at_b, 0, 2 * stations - 1)
+    turn = lax.rem(lax.broadcasted_iota(jnp.int32, (block, freq), 1), 4)
+    swap_lanes = lax.rem(turn, 2) == 0
+    sign_re = jnp.where((turn == 0) | (turn == 3), 1.0, -1.0)[:1].astype(BF16)
+    sign_im = jnp.where(turn >= 2, 1.0, -1.0)[:1].astype(BF16)
+    for copy in sends:
+        copy.wait()
+
+    def pair_body(p, carry):
+        a = near[places[0, p]].astype(F32)
+        b = near[places[1, p]].astype(F32)
         re = a[0] * b[0] + a[1] * b[1]
         im = a[1] * b[0] - a[0] * b[1]
-        rows = pl.ds(pl.multiple_of(p * block, block), block)
-        cross[rows, :freq] = re.astype(BF16)
-        cross[rows, freq:] = im.astype(BF16)
+        re, im = re.astype(BF16), im.astype(BF16)
+        low = pl.ds(pl.multiple_of(p * block, block), block)
+        high = pl.ds(pl.multiple_of(count + p * block, block), block)
+        cross[high, :freq] = re
+        cross[high, freq:] = im
+        cross[low, :freq] = jnp.where(swap_lanes, im, re) * sign_re
+        cross[low, freq:] = jnp.where(swap_lanes, re, im) * sign_im
         return carry
 
-    lax.fori_loop(0, pairs, pair_body, 0, unroll=2)
-    fill.wait()
+    lax.fori_loop(0, pairs, pair_body, 0, unroll=3)
+    for copy in fills:
+        copy.wait()
     tile = 256
 
-    for h in range(2):
-
-        def lag_body(n, carry, h=h):
-            columns = pl.ds(pl.multiple_of(n * tile, tile), tile)
-            source = pl.ds(pl.multiple_of(h * half + n * tile, tile), tile)
-            y = jnp.dot(cross[...], table[:, source], preferred_element_type=F32)
-            hi, lo = split(y)
-            vhi[h, :count, columns] = hi
-            vlo[h, :count, columns] = lo
-            return carry
-
-        lax.fori_loop(0, half // tile, lag_body, 0)
-
-    gram = None
-    for h in range(2):
-        hi, lo = vhi[h], vlo[h]
-        term = nt(hi, hi) + nt(lo, hi) + nt(hi, lo)
-        gram = term if gram is None else gram + term
+    def lag_body(n, carry):
+        y = jnp.dot(
+            cross[...],
+            table[:, pl.ds(pl.multiple_of(n * tile, tile), tile)],
+            preferred_element_type=F32,
+        ).astype(BF16)
+        held_rows[:count, pl.ds(pl.multiple_of(n * tile, tile), tile)] = y[:count]
+        held_rows[:count, pl.ds(pl.multiple_of(half + n * tile, tile), tile)] = y[count:]
+        return carry
+
+    lax.fori_loop(0, half // tile, lag_body, 0)
+    gram = nt(held_rows[...], held_rows[...])
     lane = lax.broadcasted_iota(jnp.int32, (1, 128), 1)
     group = lax.div(lax.broadcasted_iota(jnp.int32, (1, 256), 1), 8)
     row_batch = lax.div(lax.broadcasted_iota(jnp.int32, (count, 1), 0), 8)
@@ -334,43 +344,56 @@
                 columns = slice(side * 128, (side + 1) * 128)
                 coef[start : start + each, columns] = total[c * each : (c + 1) * each]
 
-    chi, clo = split(coef[...])
-    for h in range(2):
-        for n in range(half // 512):
-            a, b = vhi[h, :, n * 512 : (n + 1) * 512], vlo[h, :, n * 512 : (n + 1) * 512]
-            out = (
-                jnp.dot(chi, a, preferred_element_type=F32)
-                + jnp.dot(clo, a, preferred_element_type=F32)
-                + jnp.dot(chi, b, preferred_element_type=F32)
+    coefs = jnp.concatenate(split(coef[...]), 0)
+    size = coef.shape[0]
+    width = lags // chips
+    chunk = across * width
+    row, column = lax.div(chip, across), lax.rem(chip, across)
+    rows_order = sorted(range(other_side), key=lambda d: -min(d, other_side - d))
+    columns_order = sorted(range(across), key=lambda d: -min(d, across - d))
+    swaps, sends, merged = [], [], None
+
+    def scatter(i):
+        kept = None
+        swaps[i].wait()
+        for dy in columns_order:
+            goal_column = lax.rem(column + dy, across)
+            lanes = pl.ds(pl.multiple_of(goal_column * width, width), width)
+            block_sum = part[i, core, :, lanes] + sib[i, :, lanes]
+            if rows_order[i] == 0 and dy == 0:
+                kept = block_sum
+                continue
+            index = len(sends)
+            outgoing[index] = block_sum.astype(BF16)
+            goal = across * lax.rem(row + rows_order[i], other_side) + goal_column
+            copy = pltpu.make_async_remote_copy(
+                src_ref=outgoing.at[index], dst_ref=incoming.at[index],
+                send_sem=out_send.at[index], recv_sem=in_recv.at[index],
+                device_id={"hours": 2 * goal + core}, device_id_type=MESH,
             )
-            columns = slice(h * half + n * 512, h * half + (n + 1) * 512)
-            ws_ref[:, columns] = out[:batches]
-            for c in range(2):
-                part[c, :, columns] = out[batches + c * slots : batches + (c + 1) * slots]
-
-
-    width = lags // chips
-    swap = pltpu.make_async_remote_copy(
-        src_ref=part.at[1 - core], dst_ref=sib, send_sem=send_sem.at[2], recv_sem=recv_sem.at[2],
-        device_id=twin, device_id_type=MESH,
-    )
-    swap.start()
-    swap.wait()
-    for q in range(chips):
-        columns = slice(q * width, (q + 1) * width)
-        keep[q] = part[core, :, columns] + sib[:, columns]
-        outgoing[q] = keep[q].astype(BF16)
-    sends = []
-    for index, goal in enumerate(goals):
+            copy.start()
+            sends.append(copy)
+        return kept
+
+    for i, dx in enumerate(rows_order):
+        goal_row = lax.rem(row + dx, other_side)
+        columns = pl.ds(pl.multiple_of(goal_row * chunk, chunk), chunk)
+        out = jnp.dot(coefs, held_rows[:, columns], preferred_element_type=F32)
+        out = out[:size] + out[size:]
+        ws_ref[:, columns] = out[:batches]
+        for c in range(2):
+            part[i, c] = out[batches + c * slots : batches + (c + 1) * slots]
         copy = pltpu.make_async_remote_copy(
-            src_ref=outgoing.at[goal], dst_ref=incoming.at[index],
-            send_sem=out_send.at[index], recv_sem=in_recv.at[index],
-            device_id={"hours": 2 * goal + core}, device_id_type=MESH,
+            src_ref=part.at[i, 1 - core], dst_ref=sib.at[i],
+            send_sem=send_sem.at[i], recv_sem=recv_sem.at[i],
+            device_id=twin, device_id_type=MESH,
         )
         copy.start()
-        sends.append(copy)
-    merged = keep[chip]
-    for copy in reversed(sends):
+        swaps.append(copy)
+        if i > 0:
+            scatter(i - 1)
+    merged = scatter(other_side - 1)
+    for copy in sends:
         copy.wait()
     for index in range(chips - 1):
         merged = merged + incoming[index].astype(F32)
@@ -407,7 +430,7 @@
     fin[RANK * each :] = summed_rows[RANK * each :]
 
     last = pltpu.make_async_remote_copy(
-        src_ref=fin, dst_ref=theirs, send_sem=send_sem.at[3], recv_sem=recv_sem.at[3],
+        src_ref=fin, dst_ref=theirs, send_sem=send_sem.at[other_side], recv_sem=recv_sem.at[other_side],
         device_id=twin, device_id_type=MESH,
     )
     last.start()
@@ -447,6 +470,7 @@
     slots = 32
     chips = lax.axis_size("hours") // 2
     width = lags // chips
+    rows_of_chips = torus_offsets(chips)[1]
     raw = spectra.reshape(stations, block, 2, freq)
     vmem = pl.BlockSpec(memory_space=pltpu.VMEM)
     windows_out, merged = pl.pallas_call(
@@ -469,18 +493,17 @@
             pltpu.VMEM((2, stations // 2, 2, block, freq), BF16),
             pltpu.SMEM((2, stations // 2), jnp.int32),
             pltpu.SMEM((2, stations // 2), jnp.int32),
+            pltpu.SMEM((2, pairs), jnp.int32),
             pltpu.VMEM((2 * stations, 2, block, freq), BF16),
-            pltpu.VMEM((count, 2 * freq), BF16),
-            pltpu.VMEM((2 * freq, lags), BF16),
-            pltpu.VMEM((2, 256, half), BF16),
-            pltpu.VMEM((2, 256, half), BF16),
+            pltpu.VMEM((2 * count, 2 * freq), BF16),
+            pltpu.VMEM((2 * freq, half), BF16),
+            pltpu.VMEM((256, lags), BF16),
             pltpu.VMEM((count, 128), F32),
             pltpu.VMEM((2, batches, 128), F32),
             pltpu.VMEM((batches + 2 * slots, 256), F32),
-            pltpu.VMEM((2, slots, lags), F32),
-            pltpu.VMEM((slots, lags), F32),
-            pltpu.VMEM((chips, slots, width), F32),
-            pltpu.VMEM((chips, slots, width), BF16),
+            pltpu.VMEM((rows_of_chips, 2, slots, lags // rows_of_chips), F32),
+            pltpu.VMEM((rows_of_chips, slots, lags // rows_of_chips), F32),
+            pltpu.VMEM((chips - 1, slots, width), BF16),
             pltpu.VMEM((chips - 1, slots, width), BF16),
             pltpu.VMEM((slots, width), F32),
             pltpu.VMEM((chips, 8, 128), F32),
@@ -490,9 +513,10 @@
             pltpu.SemaphoreType.DMA((2,)),
             pltpu.SemaphoreType.DMA((2, stations // 2)),
             pltpu.SemaphoreType.DMA((2, stations // 2)),
+            pltpu.SemaphoreType.DMA((rows_of_chips + 1,)),
+            pltpu.SemaphoreType.DMA((rows_of_chips + 1,)),
+            pltpu.SemaphoreType.DMA((5,)),
             pltpu.SemaphoreType.DMA((4,)),
-            pltpu.SemaphoreType.DMA((4,)),
-            pltpu.SemaphoreType.DMA((5,)),
             pltpu.SemaphoreType.DMA((chips - 1,)),
             pltpu.SemaphoreType.DMA((chips - 1,)),
             pltpu.SemaphoreType.DMA((chips - 1,)),
@@ -527,7 +551,7 @@
     out_specs = (P("pairs", "hours", None), P("pairs", "hours"), P("pairs", None, "hours"))
 
     def whole(spectra, masks, pair_rows, start_basis):
-        table = jnp.asarray(full_table(spectra.shape[4], start_basis.shape[1]))
+        table = jnp.asarray(half_table(spectra.shape[4], start_basis.shape[1] // 2))
         return jax.shard_map(
             on_device, mesh=mesh, in_specs=(P(), *in_specs), out_specs=out_specs, check_vma=False
         )(table, spectra, masks, pair_rows, start_basis)

time: 46.7 us -> 44.7 us (0.957)
  Pallas kernels: 45.9 us -> 44 us
    pallas_call x1, Pallas kernels: 45.2 us -> 43.2 us  [on_device(): pl.pallas_call(functools.partial(station_kernel, stations, segments, wind...]
where the time goes in v5:
time: 44.7 us; the launch traced here: 44.6 us
  Pallas kernels  44 us (98%)
  between operations  0.64 us (1%)
    pallas_call x1, Pallas kernels, on_device(): pl.pallas_call(functools.partial(station_kernel, stations, segments, wind...  43.2 us

profile of v5, /device:TPU:1, one launch (start us, length us, event | category | flops | bytes accessed | tf_op | source)
XLA Modules:
  0.0 44.6 jit_solution(3062412651162794110)
XLA Ops:
  0.6 43.2 %station_pairs.1 = (f32[24,2048]{1,0:T(8,128)S(1)}, f32[2,32,64]{2,1,0:T(8,128)S(1)}) custom-call(s32[2,12]{1,0:T(2,128)} %bitcast.3, s32[8,2,8]{2,1,0:T(2,128)} %masks_hbm.1, bf16[8,16,2,1024]{3,2,1,0:T(2,128)(2,1)} %bitcast.2, bf16[2048,1024]{1,0:T(8,128)(2,1)} %constant.2.clone.table_ref, f32[4,2048]{1,0:T(4,128)} %start_hbm.1), custom_call_target="tpu_custom_call" | custom-call | tf_op jit(solution)/shard_map/station_pairs/pallas_call | solution.py:476
  43.9 0.7 %outputs.1 = (f32[12,2,2048]{2,1,0:T(2,128)}, f32[12,64]{1,0:T(8,128)}, f32[12,4,64]{2,1,0:T(4,128)}) custom-call(f32[24,2048]{1,0:T(8,128)S(1)} %get-tuple-element.5.windows_ref, f32[2,32,64]{2,1,0:T(8,128)S(1)} %get-tuple-element.6.merged_ref), custom_call_target="tpu_custom_call" | custom-call | tf_op jit(solution)/shard_map/outputs/pallas_call | solution.py:530

commit v6 on v5

--- a/solution.py
+++ b/solution.py
@@ -94,7 +94,7 @@
     ws_ref, out_ref,
     rows_ref, masks_ref, start_ref, raw, mine, packed, wants, asked, places, near,
     cross, table, held_rows, square, wide, coef,
-    part, sib, outgoing, incoming, summed_rows, grams, fin, theirs,
+    part, incoming, summed_rows, theirs, own_gram, grams,
     list_send, list_recv, halo_send, halo_recv, send_sem, recv_sem, own_sem, fill_sem,
     out_send, in_recv, gram_send, gram_recv,
 ):
@@ -132,14 +132,18 @@
     core, chip = lax.rem(hour, 2), lax.div(hour, 2)
     twin = {"hours": hour + 1 - 2 * core}
     across, other_side, offsets = torus_offsets(chips)
-    goals = [
-        across * lax.rem(lax.div(chip, across) + dx, other_side)
-        + lax.rem(lax.rem(chip, across) + dy, across)
-        for dx, dy in offsets
-    ]
+    row, column = lax.div(chip, across), lax.rem(chip, across)
+    places_from = [(dx, dy, flip) for dx, dy in offsets + [(0, 0)] for flip in range(2)][:-2]
+    places_from.append((0, 0, 1))
+
+    def device(place):
+        dx, dy, flip = place
+        goal = across * lax.rem(row + dx, other_side) + lax.rem(column + dy, across)
+        return {"hours": 2 * goal + (core if flip == 0 else 1 - core)}
+
     barrier = pltpu.get_barrier_semaphore()
-    partners = [{"pairs": before}, {"pairs": after}, twin]
-    partners += [{"hours": 2 * goal + core} for goal in goals]
+    partners = [{"pairs": before}, {"pairs": after}]
+    partners += [device(place) for place in places_from]
     for other in partners:
         pl.semaphore_signal(barrier, inc=1, device_id=other, device_id_type=MESH)
 
@@ -348,33 +352,9 @@
     size = coef.shape[0]
     width = lags // chips
     chunk = across * width
-    row, column = lax.div(chip, across), lax.rem(chip, across)
     rows_order = sorted(range(other_side), key=lambda d: -min(d, other_side - d))
     columns_order = sorted(range(across), key=lambda d: -min(d, across - d))
-    swaps, sends, merged = [], [], None
-
-    def scatter(i):
-        kept = None
-        swaps[i].wait()
-        for dy in columns_order:
-            goal_column = lax.rem(column + dy, across)
-            lanes = pl.ds(pl.multiple_of(goal_column * width, width), width)
-            block_sum = part[i, core, :, lanes] + sib[i, :, lanes]
-            if rows_order[i] == 0 and dy == 0:
-                kept = block_sum
-                continue
-            index = len(sends)
-            outgoing[index] = block_sum.astype(BF16)
-            goal = across * lax.rem(row + rows_order[i], other_side) + goal_column
-            copy = pltpu.make_async_remote_copy(
-                src_ref=outgoing.at[index], dst_ref=incoming.at[index],
-                send_sem=out_send.at[index], recv_sem=in_recv.at[index],
-                device_id={"hours": 2 * goal + core}, device_id_type=MESH,
-            )
-            copy.start()
-            sends.append(copy)
-        return kept
-
+    sends = []
     for i, dx in enumerate(rows_order):
         goal_row = lax.rem(row + dx, other_side)
         columns = pl.ds(pl.multiple_of(goal_row * chunk, chunk), chunk)
@@ -382,66 +362,76 @@
         out = out[:size] + out[size:]
         ws_ref[:, columns] = out[:batches]
         for c in range(2):
-            part[i, c] = out[batches + c * slots : batches + (c + 1) * slots]
+            block_rows = out[batches + c * slots : batches + (c + 1) * slots].astype(BF16)
+            for y in range(across):
+                part[i, c, y] = block_rows[:, y * width : (y + 1) * width]
+        for dy in columns_order:
+            for flip in range(2):
+                if (dx, dy, flip) == (0, 0, 0):
+                    continue
+                index = places_from.index((dx, dy, flip))
+                copy = pltpu.make_async_remote_copy(
+                    src_ref=part.at[
+                        i, core if flip == 0 else 1 - core, lax.rem(column + dy, across)
+                    ],
+                    dst_ref=incoming.at[index],
+                    send_sem=out_send.at[index], recv_sem=in_recv.at[index],
+                    device_id=device((dx, dy, flip)), device_id_type=MESH,
+                )
+                copy.start()
+                sends.append((index, copy))
+    merged = part[other_side - 1, core, column].astype(F32)
+    for index, copy in sends:
+        copy.wait()
+        merged = merged + incoming[index].astype(F32)
+    summed_rows[...] = merged
+
+    swap = pltpu.make_async_remote_copy(
+        src_ref=summed_rows, dst_ref=theirs, send_sem=send_sem.at[0], recv_sem=recv_sem.at[0],
+        device_id=twin, device_id_type=MESH,
+    )
+    swap.start()
+    vectors = [summed_rows[r * each : (r + 1) * each] for r in range(RANK)]
+    order = [(i, j) for i in range(RANK) for j in range(i + 1)]
+    line = lax.broadcasted_iota(jnp.int32, (each, 128), 1)
+    pair_of = lax.broadcasted_iota(jnp.int32, (each, 128), 0)
+    marks = [line == 8 * index + pair_of for index in range(len(order))]
+    tile = jnp.zeros((each, 128), F32)
+    for mark, (i, j) in zip(marks, order):
+        tile = jnp.where(mark, jnp.sum(vectors[i] * vectors[j], axis=1, keepdims=True), tile)
+    own_gram[...] = jnp.sum(tile, axis=0, keepdims=True)
+    tells = []
+    for index, place in enumerate(places_from):
         copy = pltpu.make_async_remote_copy(
-            src_ref=part.at[i, 1 - core], dst_ref=sib.at[i],
-            send_sem=send_sem.at[i], recv_sem=recv_sem.at[i],
-            device_id=twin, device_id_type=MESH,
+            src_ref=own_gram, dst_ref=grams.at[index],
+            send_sem=gram_send.at[index], recv_sem=gram_recv.at[index],
+            device_id=device(place), device_id_type=MESH,
         )
         copy.start()
-        swaps.append(copy)
-        if i > 0:
-            scatter(i - 1)
-    merged = scatter(other_side - 1)
-    for copy in sends:
+        tells.append(copy)
+    swap.wait()
+    for copy in reversed(tells):
         copy.wait()
-    for index in range(chips - 1):
-        merged = merged + incoming[index].astype(F32)
-    summed_rows[...] = merged
-    vectors = [summed_rows[r * each : (r + 1) * each] for r in range(RANK)]
-    lane = lax.broadcasted_iota(jnp.int32, (1, 128), 1)
-    tile = jnp.zeros((each, 128), F32)
-    order = [(i, j) for i in range(RANK) for j in range(i + 1)]
-    for index, (i, j) in enumerate(order):
-        value = jnp.sum(vectors[i] * vectors[j], axis=1, keepdims=True)
-        tile = tile + jnp.where(lane == index, value, 0.0)
-    grams[chips - 1, :each] = tile
-
-    sends = []
-    for index, goal in enumerate(goals):
-        copy = pltpu.make_async_remote_copy(
-            src_ref=grams.at[chips - 1], dst_ref=grams.at[index],
-            send_sem=gram_send.at[index], recv_sem=gram_recv.at[index],
-            device_id={"hours": 2 * goal + core}, device_id_type=MESH,
-        )
-        copy.start()
-        sends.append(copy)
-    for copy in reversed(sends):
-        copy.wait()
-    summed = grams[0, :each]
-    for q in range(1, chips):
-        summed = summed + grams[q, :each]
-    small = [[None] * RANK for _ in range(RANK)]
-    for index, (i, j) in enumerate(order):
-        small[i][j] = summed[:, index : index + 1]
-    result = solve(cholesky(small), vectors)
-    for r in range(RANK):
-        fin[r * each : (r + 1) * each] = result[r] * math.sqrt(lags)
-    fin[RANK * each :] = summed_rows[RANK * each :]
-
-    last = pltpu.make_async_remote_copy(
-        src_ref=fin, dst_ref=theirs, send_sem=send_sem.at[other_side], recv_sem=recv_sem.at[other_side],
-        device_id=twin, device_id_type=MESH,
-    )
-    last.start()
+    gram_sums = [own_gram[...], None]
+    for index, (_, _, flip) in enumerate(places_from):
+        value = grams[index]
+        gram_sums[flip] = value if gram_sums[flip] is None else gram_sums[flip] + value
     own_half = width // 2
 
     def halved(x):
         return jnp.where(core == 0, x[:, :own_half], x[:, own_half:])
 
-    out_ref[core] = halved(fin[...])
-    last.wait()
-    out_ref[1 - core] = halved(theirs[...])
+    for flip, source in enumerate((summed_rows, theirs)):
+        target = core if flip == 0 else 1 - core
+        small = [[None] * RANK for _ in range(RANK)]
+        for mark, (i, j) in zip(marks, order):
+            small[i][j] = jnp.sum(
+                jnp.where(mark, gram_sums[flip], 0.0), axis=1, keepdims=True
+            )
+        pieces = [halved(source[r * each : (r + 1) * each]) for r in range(RANK)]
+        for r, value in enumerate(solve(cholesky(small), pieces)):
+            out_ref[target, r * each : (r + 1) * each] = value * math.sqrt(lags)
+        out_ref[target, RANK * each :] = halved(source[RANK * each :])
 
 
 def finish_kernel(pairs, windows, windows_ref, merged_ref, ws_ref, stack_ref, basis_ref):
@@ -501,26 +491,24 @@
             pltpu.VMEM((count, 128), F32),
             pltpu.VMEM((2, batches, 128), F32),
             pltpu.VMEM((batches + 2 * slots, 256), F32),
-            pltpu.VMEM((rows_of_chips, 2, slots, lags // rows_of_chips), F32),
-            pltpu.VMEM((rows_of_chips, slots, lags // rows_of_chips), F32),
-            pltpu.VMEM((chips - 1, slots, width), BF16),
-            pltpu.VMEM((chips - 1, slots, width), BF16),
-            pltpu.VMEM((slots, width), F32),
-            pltpu.VMEM((chips, 8, 128), F32),
+            pltpu.VMEM((rows_of_chips, 2, chips // rows_of_chips, slots, width), BF16),
+            pltpu.VMEM((2 * chips - 1, slots, width), BF16),
             pltpu.VMEM((slots, width), F32),
             pltpu.VMEM((slots, width), F32),
+            pltpu.VMEM((1, 128), F32),
+            pltpu.VMEM((2 * chips - 1, 1, 128), F32),
             pltpu.SemaphoreType.DMA((2,)),
             pltpu.SemaphoreType.DMA((2,)),
             pltpu.SemaphoreType.DMA((2, stations // 2)),
             pltpu.SemaphoreType.DMA((2, stations // 2)),
-            pltpu.SemaphoreType.DMA((rows_of_chips + 1,)),
-            pltpu.SemaphoreType.DMA((rows_of_chips + 1,)),
+            pltpu.SemaphoreType.DMA((1,)),
+            pltpu.SemaphoreType.DMA((1,)),
             pltpu.SemaphoreType.DMA((5,)),
             pltpu.SemaphoreType.DMA((4,)),
-            pltpu.SemaphoreType.DMA((chips - 1,)),
-            pltpu.SemaphoreType.DMA((chips - 1,)),
-            pltpu.SemaphoreType.DMA((chips - 1,)),
-            pltpu.SemaphoreType.DMA((chips - 1,)),
+            pltpu.SemaphoreType.DMA((2 * chips - 1,)),
+            pltpu.SemaphoreType.DMA((2 * chips - 1,)),
+            pltpu.SemaphoreType.DMA((2 * chips - 1,)),
+            pltpu.SemaphoreType.DMA((2 * chips - 1,)),
         ],
         compiler_params=pltpu.CompilerParams(
             collective_id=0, has_side_effects=True, vmem_limit_bytes=60 << 20

time: 44.7 us -> 42.9 us (0.960)
  Pallas kernels: 44 us -> 42.2 us
    pallas_call x1, Pallas kernels: 43.2 us -> 41.4 us  [on_device(): pl.pallas_call(functools.partial(station_kernel, stations, segments, wind...]
where the time goes in v6:
time: 42.9 us; the launch traced here: 42.8 us
  Pallas kernels  42.2 us (98%)
  between operations  0.64 us (1%)
    pallas_call x1, Pallas kernels, on_device(): pl.pallas_call(functools.partial(station_kernel, stations, segments, wind...  41.4 us

profile of v6, /device:TPU:1, one launch (start us, length us, event | category | flops | bytes accessed | tf_op | source)
XLA Modules:
  0.0 42.8 jit_solution(30603603984464193)
XLA Ops:
  0.6 41.4 %station_pairs.1 = (f32[24,2048]{1,0:T(8,128)S(1)}, f32[2,32,64]{2,1,0:T(8,128)S(1)}) custom-call(s32[2,12]{1,0:T(2,128)} %bitcast.3, s32[8,2,8]{2,1,0:T(2,128)} %masks_hbm.1, bf16[8,16,2,1024]{3,2,1,0:T(2,128)(2,1)} %bitcast.2, bf16[2048,1024]{1,0:T(8,128)(2,1)} %constant.2.clone.table_ref, f32[4,2048]{1,0:T(4,128)} %start_hbm.1), custom_call_target="tpu_custom_call" | custom-call | tf_op jit(solution)/shard_map/station_pairs/pallas_call | solution.py:466
  42.1 0.7 %outputs.1 = (f32[12,2,2048]{2,1,0:T(2,128)}, f32[12,64]{1,0:T(8,128)}, f32[12,4,64]{2,1,0:T(4,128)}) custom-call(f32[24,2048]{1,0:T(8,128)S(1)} %get-tuple-element.5.windows_ref, f32[2,32,64]{2,1,0:T(8,128)S(1)} %get-tuple-element.6.merged_ref), custom_call_target="tpu_custom_call" | custom-call | tf_op jit(solution)/shard_map/outputs/pallas_call | solution.py:518

commit v7 on v6

--- a/solution.py
+++ b/solution.py
@@ -56,7 +56,7 @@
             total = gram[row][col]
             for inner in range(col):
                 total = total - lower[row][inner] * lower[col][inner]
-            lower[row][col] = jnp.sqrt(total) if row == col else total / lower[col][col]
+            lower[row][col] = 1.0 / jnp.sqrt(total) if row == col else total * lower[col][col]
     return lower
 
 
@@ -66,7 +66,7 @@
         current = vectors[row]
         for inner in range(row):
             current = current - lower[row][inner] * result[inner]
-        result.append(current / lower[row][row])
+        result.append(current * lower[row][row])
     return result
 
 
@@ -273,7 +273,7 @@
         return carry
 
     lax.fori_loop(0, half // tile, lag_body, 0)
-    gram = nt(held_rows[...], held_rows[...])
+    gram = nt(held_rows[: count + 16], held_rows[...])
     lane = lax.broadcasted_iota(jnp.int32, (1, 128), 1)
     group = lax.div(lax.broadcasted_iota(jnp.int32, (1, 256), 1), 8)
     row_batch = lax.div(lax.broadcasted_iota(jnp.int32, (count, 1), 0), 8)
@@ -360,7 +360,6 @@
         columns = pl.ds(pl.multiple_of(goal_row * chunk, chunk), chunk)
         out = jnp.dot(coefs, held_rows[:, columns], preferred_element_type=F32)
         out = out[:size] + out[size:]
-        ws_ref[:, columns] = out[:batches]
         for c in range(2):
             block_rows = out[batches + c * slots : batches + (c + 1) * slots].astype(BF16)
             for y in range(across):
@@ -380,9 +379,10 @@
                 )
                 copy.start()
                 sends.append((index, copy))
+        ws_ref[:, columns] = out[:batches]
     merged = part[other_side - 1, core, column].astype(F32)
-    for index, copy in sends:
-        copy.wait()
+    for index, copy in reversed(sends):
+        copy.wait_recv()
         merged = merged + incoming[index].astype(F32)
     summed_rows[...] = merged
 
@@ -410,10 +410,12 @@
         copy.start()
         tells.append(copy)
     swap.wait()
-    for copy in reversed(tells):
-        copy.wait()
+    for _, copy in sends:
+        copy.wait_send()
     gram_sums = [own_gram[...], None]
-    for index, (_, _, flip) in enumerate(places_from):
+    for index in reversed(range(len(tells))):
+        tells[index].wait_recv()
+        flip = places_from[index][2]
         value = grams[index]
         gram_sums[flip] = value if gram_sums[flip] is None else gram_sums[flip] + value
     own_half = width // 2
@@ -432,6 +434,8 @@
         for r, value in enumerate(solve(cholesky(small), pieces)):
             out_ref[target, r * each : (r + 1) * each] = value * math.sqrt(lags)
         out_ref[target, RANK * each :] = halved(source[RANK * each :])
+    for copy in tells:
+        copy.wait_send()
 
 
 def finish_kernel(pairs, windows, windows_ref, merged_ref, ws_ref, stack_ref, basis_ref):

time: 42.9 us -> 43 us (level)
  no operation moved by 1% of the time
where the time goes in v7:
time: 43 us; the launch traced here: 42.9 us
  Pallas kernels  42.2 us (98%)
  between operations  0.64 us (1%)
    pallas_call x1, Pallas kernels, on_device(): pl.pallas_call(functools.partial(station_kernel, stations, segments, wind...  41.5 us

profile of v7, /device:TPU:1, one launch (start us, length us, event | category | flops | bytes accessed | tf_op | source)
XLA Modules:
  0.0 42.9 jit_solution(739126308563631021)
XLA Ops:
  0.6 41.5 %station_pairs.1 = (f32[24,2048]{1,0:T(8,128)S(1)}, f32[2,32,64]{2,1,0:T(8,128)S(1)}) custom-call(s32[2,12]{1,0:T(2,128)} %bitcast.3, s32[8,2,8]{2,1,0:T(2,128)} %masks_hbm.1, bf16[8,16,2,1024]{3,2,1,0:T(2,128)(2,1)} %bitcast.2, bf16[2048,1024]{1,0:T(8,128)(2,1)} %constant.2.clone.table_ref, f32[4,2048]{1,0:T(4,128)} %start_hbm.1), custom_call_target="tpu_custom_call" | custom-call | tf_op jit(solution)/shard_map/station_pairs/pallas_call | solution.py:470
  42.1 0.7 %outputs.1 = (f32[12,2,2048]{2,1,0:T(2,128)}, f32[12,64]{1,0:T(8,128)}, f32[12,4,64]{2,1,0:T(4,128)}) custom-call(f32[24,2048]{1,0:T(8,128)S(1)} %get-tuple-element.5.windows_ref, f32[2,32,64]{2,1,0:T(8,128)S(1)} %get-tuple-element.6.merged_ref), custom_call_target="tpu_custom_call" | custom-call | tf_op jit(solution)/shard_map/outputs/pallas_call | solution.py:522

commit v8 on v7

--- a/solution.py
+++ b/solution.py
@@ -94,7 +94,7 @@
     ws_ref, out_ref,
     rows_ref, masks_ref, start_ref, raw, mine, packed, wants, asked, places, near,
     cross, table, held_rows, square, wide, coef,
-    part, incoming, summed_rows, theirs, own_gram, grams,
+    part, sib, outgoing, incoming, summed_rows, theirs, own_gram, grams,
     list_send, list_recv, halo_send, halo_recv, send_sem, recv_sem, own_sem, fill_sem,
     out_send, in_recv, gram_send, gram_recv,
 ):
@@ -260,7 +260,7 @@
     lax.fori_loop(0, pairs, pair_body, 0, unroll=3)
     for copy in fills:
         copy.wait()
-    tile = 256
+    tile = 512
 
     def lag_body(n, carry):
         y = jnp.dot(
@@ -354,40 +354,54 @@
     chunk = across * width
     rows_order = sorted(range(other_side), key=lambda d: -min(d, other_side - d))
     columns_order = sorted(range(across), key=lambda d: -min(d, across - d))
-    sends = []
+    swaps, sends = [], []
+
+    def scatter(i):
+        kept = None
+        swaps[i].wait_recv()
+        for dy in columns_order:
+            goal_column = lax.rem(column + dy, across)
+            lanes = pl.ds(pl.multiple_of(goal_column * width, width), width)
+            block_sum = part[i, core, :, lanes] + sib[i, :, lanes]
+            if rows_order[i] == 0 and dy == 0:
+                kept = block_sum
+                continue
+            index = len(sends)
+            outgoing[index] = block_sum.astype(BF16)
+            copy = pltpu.make_async_remote_copy(
+                src_ref=outgoing.at[index], dst_ref=incoming.at[index],
+                send_sem=out_send.at[index], recv_sem=in_recv.at[index],
+                device_id=device((rows_order[i], dy, 0)), device_id_type=MESH,
+            )
+            copy.start()
+            sends.append(copy)
+        return kept
+
     for i, dx in enumerate(rows_order):
         goal_row = lax.rem(row + dx, other_side)
         columns = pl.ds(pl.multiple_of(goal_row * chunk, chunk), chunk)
         out = jnp.dot(coefs, held_rows[:, columns], preferred_element_type=F32)
         out = out[:size] + out[size:]
         for c in range(2):
-            block_rows = out[batches + c * slots : batches + (c + 1) * slots].astype(BF16)
-            for y in range(across):
-                part[i, c, y] = block_rows[:, y * width : (y + 1) * width]
-        for dy in columns_order:
-            for flip in range(2):
-                if (dx, dy, flip) == (0, 0, 0):
-                    continue
-                index = places_from.index((dx, dy, flip))
-                copy = pltpu.make_async_remote_copy(
-                    src_ref=part.at[
-                        i, core if flip == 0 else 1 - core, lax.rem(column + dy, across)
-                    ],
-                    dst_ref=incoming.at[index],
-                    send_sem=out_send.at[index], recv_sem=in_recv.at[index],
-                    device_id=device((dx, dy, flip)), device_id_type=MESH,
-                )
-                copy.start()
-                sends.append((index, copy))
+            part[i, c] = out[batches + c * slots : batches + (c + 1) * slots]
+        copy = pltpu.make_async_remote_copy(
+            src_ref=part.at[i, 1 - core], dst_ref=sib.at[i],
+            send_sem=send_sem.at[i], recv_sem=recv_sem.at[i],
+            device_id=twin, device_id_type=MESH,
+        )
+        copy.start()
+        swaps.append(copy)
         ws_ref[:, columns] = out[:batches]
-    merged = part[other_side - 1, core, column].astype(F32)
-    for index, copy in reversed(sends):
-        copy.wait_recv()
+        if i > 0:
+            scatter(i - 1)
+    merged = scatter(other_side - 1)
+    for index in reversed(range(len(sends))):
+        sends[index].wait_recv()
         merged = merged + incoming[index].astype(F32)
     summed_rows[...] = merged
 
     swap = pltpu.make_async_remote_copy(
-        src_ref=summed_rows, dst_ref=theirs, send_sem=send_sem.at[0], recv_sem=recv_sem.at[0],
+        src_ref=summed_rows, dst_ref=theirs, send_sem=send_sem.at[other_side], recv_sem=recv_sem.at[other_side],
         device_id=twin, device_id_type=MESH,
     )
     swap.start()
@@ -410,7 +424,7 @@
         copy.start()
         tells.append(copy)
     swap.wait()
-    for _, copy in sends:
+    for copy in swaps + sends:
         copy.wait_send()
     gram_sums = [own_gram[...], None]
     for index in reversed(range(len(tells))):
@@ -495,8 +509,10 @@
             pltpu.VMEM((count, 128), F32),
             pltpu.VMEM((2, batches, 128), F32),
             pltpu.VMEM((batches + 2 * slots, 256), F32),
-            pltpu.VMEM((rows_of_chips, 2, chips // rows_of_chips, slots, width), BF16),
-            pltpu.VMEM((2 * chips - 1, slots, width), BF16),
+            pltpu.VMEM((rows_of_chips, 2, slots, lags // rows_of_chips), F32),
+            pltpu.VMEM((rows_of_chips, slots, lags // rows_of_chips), F32),
+            pltpu.VMEM((chips - 1, slots, width), BF16),
+            pltpu.VMEM((chips - 1, slots, width), BF16),
             pltpu.VMEM((slots, width), F32),
             pltpu.VMEM((slots, width), F32),
             pltpu.VMEM((1, 128), F32),
@@ -505,12 +521,12 @@
             pltpu.SemaphoreType.DMA((2,)),
             pltpu.SemaphoreType.DMA((2, stations // 2)),
             pltpu.SemaphoreType.DMA((2, stations // 2)),
-            pltpu.SemaphoreType.DMA((1,)),
-            pltpu.SemaphoreType.DMA((1,)),
+            pltpu.SemaphoreType.DMA((rows_of_chips + 1,)),
+            pltpu.SemaphoreType.DMA((rows_of_chips + 1,)),
             pltpu.SemaphoreType.DMA((5,)),
             pltpu.SemaphoreType.DMA((4,)),
-            pltpu.SemaphoreType.DMA((2 * chips - 1,)),
-            pltpu.SemaphoreType.DMA((2 * chips - 1,)),
+            pltpu.SemaphoreType.DMA((chips - 1,)),
+            pltpu.SemaphoreType.DMA((chips - 1,)),
             pltpu.SemaphoreType.DMA((2 * chips - 1,)),
             pltpu.SemaphoreType.DMA((2 * chips - 1,)),
         ],

time: 43 us -> 43.4 us (level)
  Pallas kernels: 42.2 us -> 42.7 us
where the time goes in v8:
time: 43.4 us; the launch traced here: 43.3 us
  Pallas kernels  42.7 us (98%)
  between operations  0.64 us (1%)
    pallas_call x1, Pallas kernels, on_device(): pl.pallas_call(functools.partial(station_kernel, stations, segments, wind...  41.9 us

profile of v8, /device:TPU:1, one launch (start us, length us, event | category | flops | bytes accessed | tf_op | source)
XLA Modules:
  0.0 43.3 jit_solution(15370931909289432610)
XLA Ops:
  0.6 41.9 %station_pairs.1 = (f32[24,2048]{1,0:T(8,128)S(1)}, f32[2,32,64]{2,1,0:T(8,128)S(1)}) custom-call(s32[2,12]{1,0:T(2,128)} %bitcast.3, s32[8,2,8]{2,1,0:T(2,128)} %masks_hbm.1, bf16[8,16,2,1024]{3,2,1,0:T(2,128)(2,1)} %bitcast.2, bf16[2048,1024]{1,0:T(8,128)(2,1)} %constant.2.clone.table_ref, f32[4,2048]{1,0:T(4,128)} %start_hbm.1), custom_call_target="tpu_custom_call" | custom-call | tf_op jit(solution)/shard_map/station_pairs/pallas_call | solution.py:484
  42.6 0.7 %outputs.1 = (f32[12,2,2048]{2,1,0:T(2,128)}, f32[12,64]{1,0:T(8,128)}, f32[12,4,64]{2,1,0:T(4,128)}) custom-call(f32[24,2048]{1,0:T(8,128)S(1)} %get-tuple-element.5.windows_ref, f32[2,32,64]{2,1,0:T(8,128)S(1)} %get-tuple-element.6.merged_ref), custom_call_target="tpu_custom_call" | custom-call | tf_op jit(solution)/shard_map/outputs/pallas_call | solution.py:538

commit v9 on v7

--- a/solution.py
+++ b/solution.py
@@ -241,7 +241,8 @@
     sign_re = jnp.where((turn == 0) | (turn == 3), 1.0, -1.0)[:1].astype(BF16)
     sign_im = jnp.where(turn >= 2, 1.0, -1.0)[:1].astype(BF16)
     for copy in sends:
-        copy.wait()
+        copy.wait_recv()
+    halos = sends
 
     def pair_body(p, carry):
         a = near[places[0, p]].astype(F32)
@@ -260,7 +261,7 @@
     lax.fori_loop(0, pairs, pair_body, 0, unroll=3)
     for copy in fills:
         copy.wait()
-    tile = 256
+    tile = 512
 
     def lag_body(n, carry):
         y = jnp.dot(
@@ -348,8 +349,8 @@
                 columns = slice(side * 128, (side + 1) * 128)
                 coef[start : start + each, columns] = total[c * each : (c + 1) * each]
 
-    coefs = jnp.concatenate(split(coef[...]), 0)
-    size = coef.shape[0]
+    coefs = jnp.concatenate(split(coef[batches:]), 0)
+    size = coef.shape[0] - batches
     width = lags // chips
     chunk = across * width
     rows_order = sorted(range(other_side), key=lambda d: -min(d, other_side - d))
@@ -361,7 +362,7 @@
         out = jnp.dot(coefs, held_rows[:, columns], preferred_element_type=F32)
         out = out[:size] + out[size:]
         for c in range(2):
-            block_rows = out[batches + c * slots : batches + (c + 1) * slots].astype(BF16)
+            block_rows = out[c * slots : (c + 1) * slots].astype(BF16)
             for y in range(across):
                 part[i, c, y] = block_rows[:, y * width : (y + 1) * width]
         for dy in columns_order:
@@ -379,7 +380,11 @@
                 )
                 copy.start()
                 sends.append((index, copy))
-        ws_ref[:, columns] = out[:batches]
+    coefs = jnp.concatenate(split(coef[:batches]), 0)
+    for i in range(other_side):
+        columns = slice(i * chunk, (i + 1) * chunk)
+        out = jnp.dot(coefs, held_rows[:, columns], preferred_element_type=F32)
+        ws_ref[:, columns] = out[:batches] + out[batches:]
     merged = part[other_side - 1, core, column].astype(F32)
     for index, copy in reversed(sends):
         copy.wait_recv()
@@ -410,6 +415,8 @@
         copy.start()
         tells.append(copy)
     swap.wait()
+    for copy in halos:
+        copy.wait_send()
     for _, copy in sends:
         copy.wait_send()
     gram_sums = [own_gram[...], None]

time: 43 us -> 42.6 us (level)
  no operation moved by 1% of the time
where the time goes in v9:
time: 42.6 us; the launch traced here: 42.5 us
  Pallas kernels  41.9 us (98%)
  between operations  0.64 us (2%)
    pallas_call x1, Pallas kernels, on_device(): pl.pallas_call(functools.partial(station_kernel, stations, segments, wind...  41.1 us

profile of v9, /device:TPU:1, one launch (start us, length us, event | category | flops | bytes accessed | tf_op | source)
XLA Modules:
  0.0 42.5 jit_solution(499625664745861037)
XLA Ops:
  0.6 41.1 %station_pairs.1 = (f32[24,2048]{1,0:T(8,128)S(1)}, f32[2,32,64]{2,1,0:T(8,128)S(1)}) custom-call(s32[2,12]{1,0:T(2,128)} %bitcast.3, s32[8,2,8]{2,1,0:T(2,128)} %masks_hbm.1, bf16[8,16,2,1024]{3,2,1,0:T(2,128)(2,1)} %bitcast.2, bf16[2048,1024]{1,0:T(8,128)(2,1)} %constant.2.clone.table_ref, f32[4,2048]{1,0:T(4,128)} %start_hbm.1), custom_call_target="tpu_custom_call" | custom-call | tf_op jit(solution)/shard_map/station_pairs/pallas_call | solution.py:477
  41.8 0.7 %outputs.1 = (f32[12,2,2048]{2,1,0:T(2,128)}, f32[12,64]{1,0:T(8,128)}, f32[12,4,64]{2,1,0:T(4,128)}) custom-call(f32[24,2048]{1,0:T(8,128)S(1)} %get-tuple-element.5.windows_ref, f32[2,32,64]{2,1,0:T(8,128)S(1)} %get-tuple-element.6.merged_ref), custom_call_target="tpu_custom_call" | custom-call | tf_op jit(solution)/shard_map/outputs/pallas_call | solution.py:529

commit v10 on v9

--- a/solution.py
+++ b/solution.py
@@ -22,7 +22,8 @@
     shifts = np.arange(half, dtype=np.int64)[None, :]
     phase = np.mod(bins * shifts, 4 * half).astype(np.float64) * (math.pi / (2 * half))
     scale = freq ** (-0.5)
-    table = np.concatenate([np.cos(phase) * scale, -np.sin(phase) * scale], 0)
+    table = np.stack([np.cos(phase) * scale, -np.sin(phase) * scale], 0)
+    table = table.reshape(2, 2, freq // 2, half).transpose(1, 0, 2, 3).reshape(2 * freq, half)
     return table.astype(np.float32).astype(jnp.bfloat16)
 
 
@@ -92,8 +93,8 @@
     stations, segments, windows, pairs, freq, half,
     rows_hbm, masks_hbm, raw_ref, table_ref, start_hbm,
     ws_ref, out_ref,
-    rows_ref, masks_ref, start_ref, raw, mine, packed, wants, asked, places, near,
-    cross, table, held_rows, square, wide, coef,
+    rows_ref, masks_ref, start_ref, raw, mine, packed, wants, asked, places, near_low, near_high,
+    cross, first_sum, table, held_rows, square, wide, coef,
     part, incoming, summed_rows, theirs, own_gram, grams,
     list_send, list_recv, halo_send, halo_recv, send_sem, recv_sem, own_sem, fill_sem,
     out_send, in_recv, gram_send, gram_recv,
@@ -192,6 +193,8 @@
         lax.broadcasted_iota(jnp.int32, (block, segments), 0), segments
     ) == lax.broadcasted_iota(jnp.int32, (block, segments), 1)
 
+    nears, cut = (near_low, near_high), freq // 2
+
     def station_body(s, carry):
         flags = masks_ref[s].astype(F32)
         lines = jnp.concatenate(
@@ -200,24 +203,28 @@
         mask = jnp.sum(jnp.where(diagonal, lines, 0.0), axis=1, keepdims=True)
         x = jnp.swapaxes(raw[s].astype(F32), 0, 1)
         re, im = whiten(x, mask, ones)
-        mine[s, 0], mine[s, 1] = re, im
-        near[some + s, 0], near[some + s, 1] = re, im
+        for b, near in enumerate(nears):
+            bins = slice(b * cut, (b + 1) * cut)
+            mine[b, s, 0], mine[b, s, 1] = re[:, bins], im[:, bins]
+            near[some + s, 0], near[some + s, 1] = re[:, bins], im[:, bins]
         return carry
 
     lax.fori_loop(0, stations, station_body, 0, unroll=2)
-    sends = []
-    for side, other in ((1, after), (0, before)):
-        asks[1 - side].wait_recv()
-        slot = 0 if side == 1 else some + stations
+    halos = [[], []]
+    for copy in asks:
+        copy.wait_recv()
+    for b in range(2):
         for t in range(some):
-            packed[side, t] = mine[jnp.clip(asked[side, t], 0, stations - 1)]
-            copy = pltpu.make_async_remote_copy(
-                src_ref=packed.at[side, t], dst_ref=near.at[slot + t],
-                send_sem=halo_send.at[side, t], recv_sem=halo_recv.at[side, t],
-                device_id={"pairs": other}, device_id_type=MESH,
-            )
-            copy.start()
-            sends.append(copy)
+            for side, other in ((1, after), (0, before)):
+                slot = 0 if side == 1 else some + stations
+                packed[b, side, t] = mine[b, jnp.clip(asked[side, t], 0, stations - 1)]
+                copy = pltpu.make_async_remote_copy(
+                    src_ref=packed.at[b, side, t], dst_ref=nears[b].at[slot + t],
+                    send_sem=halo_send.at[b, side, t], recv_sem=halo_recv.at[b, side, t],
+                    device_id={"pairs": other}, device_id_type=MESH,
+                )
+                copy.start()
+                halos[b].append(copy)
     for copy in asks:
         copy.wait_send()
 
@@ -236,44 +243,51 @@
         at_b = jnp.where(relative == 0, low, jnp.where(relative == 1, some + local, high))
         places[0, p] = some + lax.rem(rows_ref[0, p], stations)
         places[1, p] = jnp.clip(at_b, 0, 2 * stations - 1)
-    turn = lax.rem(lax.broadcasted_iota(jnp.int32, (block, freq), 1), 4)
+    turn = lax.rem(lax.broadcasted_iota(jnp.int32, (block, cut), 1), 4)
     swap_lanes = lax.rem(turn, 2) == 0
     sign_re = jnp.where((turn == 0) | (turn == 3), 1.0, -1.0)[:1].astype(BF16)
     sign_im = jnp.where(turn >= 2, 1.0, -1.0)[:1].astype(BF16)
-    for copy in sends:
-        copy.wait_recv()
-    halos = sends
-
-    def pair_body(p, carry):
-        a = near[places[0, p]].astype(F32)
-        b = near[places[1, p]].astype(F32)
-        re = a[0] * b[0] + a[1] * b[1]
-        im = a[1] * b[0] - a[0] * b[1]
-        re, im = re.astype(BF16), im.astype(BF16)
-        low = pl.ds(pl.multiple_of(p * block, block), block)
-        high = pl.ds(pl.multiple_of(count + p * block, block), block)
-        cross[high, :freq] = re
-        cross[high, freq:] = im
-        cross[low, :freq] = jnp.where(swap_lanes, im, re) * sign_re
-        cross[low, freq:] = jnp.where(swap_lanes, re, im) * sign_im
-        return carry
-
-    lax.fori_loop(0, pairs, pair_body, 0, unroll=3)
-    for copy in fills:
-        copy.wait()
     tile = 512
-
-    def lag_body(n, carry):
-        y = jnp.dot(
-            cross[...],
-            table[:, pl.ds(pl.multiple_of(n * tile, tile), tile)],
-            preferred_element_type=F32,
-        ).astype(BF16)
-        held_rows[:count, pl.ds(pl.multiple_of(n * tile, tile), tile)] = y[:count]
-        held_rows[:count, pl.ds(pl.multiple_of(half + n * tile, tile), tile)] = y[count:]
-        return carry
-
-    lax.fori_loop(0, half // tile, lag_body, 0)
+    for b, near in enumerate(nears):
+        for copy in halos[b]:
+            copy.wait_recv()
+
+        def pair_body(p, carry, b=b, near=near):
+            x = near[places[0, p]].astype(F32)
+            y = near[places[1, p]].astype(F32)
+            re = (x[0] * y[0] + x[1] * y[1]).astype(BF16)
+            im = (x[1] * y[0] - x[0] * y[1]).astype(BF16)
+            low = pl.ds(pl.multiple_of(p * block, block), block)
+            high = pl.ds(pl.multiple_of(count + p * block, block), block)
+            reals, imags = slice(b * freq, b * freq + cut), slice(b * freq + cut, (b + 1) * freq)
+            cross[high, reals] = re
+            cross[high, imags] = im
+            cross[low, reals] = jnp.where(swap_lanes, im, re) * sign_re
+            cross[low, imags] = jnp.where(swap_lanes, re, im) * sign_im
+            return carry
+
+        lax.fori_loop(0, pairs, pair_body, 0, unroll=3)
+        if b == 0:
+            for copy in fills:
+                copy.wait()
+
+        def lag_body(n, carry, b=b):
+            lanes = pl.ds(pl.multiple_of(n * tile, tile), tile)
+            y = jnp.dot(
+                cross[:, b * freq : (b + 1) * freq],
+                table[b * freq : (b + 1) * freq, lanes],
+                preferred_element_type=F32,
+            )
+            if b == 0:
+                first_sum[:, lanes] = y
+                return carry
+            y = (y + first_sum[:, lanes]).astype(BF16)
+            held_rows[:count, lanes] = y[:count]
+            held_rows[:count, pl.ds(pl.multiple_of(half + n * tile, tile), tile)] = y[count:]
+            return carry
+
+        lax.fori_loop(0, half // tile, lag_body, 0)
+
     gram = nt(held_rows[: count + 16], held_rows[...])
     lane = lax.broadcasted_iota(jnp.int32, (1, 128), 1)
     group = lax.div(lax.broadcasted_iota(jnp.int32, (1, 256), 1), 8)
@@ -415,7 +429,7 @@
         copy.start()
         tells.append(copy)
     swap.wait()
-    for copy in halos:
+    for copy in halos[0] + halos[1]:
         copy.wait_send()
     for _, copy in sends:
         copy.wait_send()
@@ -490,13 +504,15 @@
             pltpu.VMEM((stations, windows, segments), jnp.int32),
             pltpu.VMEM((RANK, lags), F32),
             pltpu.VMEM((stations, block, 2, freq), BF16),
-            pltpu.VMEM((stations, 2, block, freq), BF16),
-            pltpu.VMEM((2, stations // 2, 2, block, freq), BF16),
+            pltpu.VMEM((2, stations, 2, block, freq // 2), BF16),
+            pltpu.VMEM((2, 2, stations // 2, 2, block, freq // 2), BF16),
             pltpu.SMEM((2, stations // 2), jnp.int32),
             pltpu.SMEM((2, stations // 2), jnp.int32),
             pltpu.SMEM((2, pairs), jnp.int32),
-            pltpu.VMEM((2 * stations, 2, block, freq), BF16),
+            pltpu.VMEM((2 * stations, 2, block, freq // 2), BF16),
+            pltpu.VMEM((2 * stations, 2, block, freq // 2), BF16),
             pltpu.VMEM((2 * count, 2 * freq), BF16),
+            pltpu.VMEM((2 * count, half), F32),
             pltpu.VMEM((2 * freq, half), BF16),
             pltpu.VMEM((256, lags), BF16),
             pltpu.VMEM((count, 128), F32),
@@ -510,8 +526,8 @@
             pltpu.VMEM((2 * chips - 1, 1, 128), F32),
             pltpu.SemaphoreType.DMA((2,)),
             pltpu.SemaphoreType.DMA((2,)),
-            pltpu.SemaphoreType.DMA((2, stations // 2)),
-            pltpu.SemaphoreType.DMA((2, stations // 2)),
+            pltpu.SemaphoreType.DMA((2, 2, stations // 2)),
+            pltpu.SemaphoreType.DMA((2, 2, stations // 2)),
             pltpu.SemaphoreType.DMA((1,)),
             pltpu.SemaphoreType.DMA((1,)),
             pltpu.SemaphoreType.DMA((5,)),

time: 42.6 us -> 41.4 us (0.972)
  Pallas kernels: 41.9 us -> 40.7 us
    pallas_call x1, Pallas kernels: 41.1 us -> 39.9 us  [on_device(): pl.pallas_call(functools.partial(station_kernel, stations, segments, wind...]
where the time goes in v10:
time: 41.4 us; the launch traced here: 41.3 us
  Pallas kernels  40.7 us (98%)
  between operations  0.64 us (2%)
    pallas_call x1, Pallas kernels, on_device(): pl.pallas_call(functools.partial(station_kernel, stations, segments, wind...  39.9 us

profile of v10, /device:TPU:1, one launch (start us, length us, event | category | flops | bytes accessed | tf_op | source)
XLA Modules:
  0.0 41.3 jit_solution(2555206156154409521)
XLA Ops:
  0.6 39.9 %station_pairs.1 = (f32[24,2048]{1,0:T(8,128)S(1)}, f32[2,32,64]{2,1,0:T(8,128)S(1)}) custom-call(s32[2,12]{1,0:T(2,128)} %bitcast.3, s32[8,2,8]{2,1,0:T(2,128)} %masks_hbm.1, bf16[8,16,2,1024]{3,2,1,0:T(2,128)(2,1)} %bitcast.2, bf16[2048,1024]{1,0:T(8,128)(2,1)} %constant.2.clone.table_ref, f32[4,2048]{1,0:T(4,128)} %start_hbm.1), custom_call_target="tpu_custom_call" | custom-call | tf_op jit(solution)/shard_map/station_pairs/pallas_call | solution.py:491
  40.6 0.7 %outputs.1 = (f32[12,2,2048]{2,1,0:T(2,128)}, f32[12,64]{1,0:T(8,128)}, f32[12,4,64]{2,1,0:T(4,128)}) custom-call(f32[24,2048]{1,0:T(8,128)S(1)} %get-tuple-element.5.windows_ref, f32[2,32,64]{2,1,0:T(8,128)S(1)} %get-tuple-element.6.merged_ref), custom_call_target="tpu_custom_call" | custom-call | tf_op jit(solution)/shard_map/outputs/pallas_call | solution.py:545

commit v11 on v10

--- a/solution.py
+++ b/solution.py
@@ -11,6 +11,7 @@
 
 BAND = 64
 TURNS = 2
+CUTS = 4
 RANK = 4
 MESH = pl.DeviceIdType.MESH
 F32 = jnp.float32
@@ -23,7 +24,7 @@
     phase = np.mod(bins * shifts, 4 * half).astype(np.float64) * (math.pi / (2 * half))
     scale = freq ** (-0.5)
     table = np.stack([np.cos(phase) * scale, -np.sin(phase) * scale], 0)
-    table = table.reshape(2, 2, freq // 2, half).transpose(1, 0, 2, 3).reshape(2 * freq, half)
+    table = table.reshape(2, CUTS, freq // CUTS, half).transpose(1, 0, 2, 3).reshape(2 * freq, half)
     return table.astype(np.float32).astype(jnp.bfloat16)
 
 
@@ -93,7 +94,7 @@
     stations, segments, windows, pairs, freq, half,
     rows_hbm, masks_hbm, raw_ref, table_ref, start_hbm,
     ws_ref, out_ref,
-    rows_ref, masks_ref, start_ref, raw, mine, packed, wants, asked, places, near_low, near_high,
+    rows_ref, masks_ref, start_ref, raw, mine, packed, wants, asked, places, near_a, near_b, near_c, near_d,
     cross, first_sum, table, held_rows, square, wide, coef,
     part, incoming, summed_rows, theirs, own_gram, grams,
     list_send, list_recv, halo_send, halo_recv, send_sem, recv_sem, own_sem, fill_sem,
@@ -193,7 +194,7 @@
         lax.broadcasted_iota(jnp.int32, (block, segments), 0), segments
     ) == lax.broadcasted_iota(jnp.int32, (block, segments), 1)
 
-    nears, cut = (near_low, near_high), freq // 2
+    nears, cut = (near_a, near_b, near_c, near_d), freq // CUTS
 
     def station_body(s, carry):
         flags = masks_ref[s].astype(F32)
@@ -210,10 +211,10 @@
         return carry
 
     lax.fori_loop(0, stations, station_body, 0, unroll=2)
-    halos = [[], []]
+    halos = [[] for _ in range(CUTS)]
     for copy in asks:
         copy.wait_recv()
-    for b in range(2):
+    for b in range(CUTS):
         for t in range(some):
             for side, other in ((1, after), (0, before)):
                 slot = 0 if side == 1 else some + stations
@@ -259,7 +260,8 @@
             im = (x[1] * y[0] - x[0] * y[1]).astype(BF16)
             low = pl.ds(pl.multiple_of(p * block, block), block)
             high = pl.ds(pl.multiple_of(count + p * block, block), block)
-            reals, imags = slice(b * freq, b * freq + cut), slice(b * freq + cut, (b + 1) * freq)
+            reals = slice(2 * b * cut, (2 * b + 1) * cut)
+            imags = slice((2 * b + 1) * cut, (2 * b + 2) * cut)
             cross[high, reals] = re
             cross[high, imags] = im
             cross[low, reals] = jnp.where(swap_lanes, im, re) * sign_re
@@ -274,14 +276,16 @@
         def lag_body(n, carry, b=b):
             lanes = pl.ds(pl.multiple_of(n * tile, tile), tile)
             y = jnp.dot(
-                cross[:, b * freq : (b + 1) * freq],
-                table[b * freq : (b + 1) * freq, lanes],
+                cross[:, 2 * b * cut : (2 * b + 2) * cut],
+                table[2 * b * cut : (2 * b + 2) * cut, lanes],
                 preferred_element_type=F32,
             )
-            if b == 0:
+            if b > 0:
+                y = y + first_sum[:, lanes]
+            if b < CUTS - 1:
                 first_sum[:, lanes] = y
                 return carry
-            y = (y + first_sum[:, lanes]).astype(BF16)
+            y = y.astype(BF16)
             held_rows[:count, lanes] = y[:count]
             held_rows[:count, pl.ds(pl.multiple_of(half + n * tile, tile), tile)] = y[count:]
             return carry
@@ -429,7 +433,7 @@
         copy.start()
         tells.append(copy)
     swap.wait()
-    for copy in halos[0] + halos[1]:
+    for copy in sum(halos, []):
         copy.wait_send()
     for _, copy in sends:
         copy.wait_send()
@@ -504,13 +508,15 @@
             pltpu.VMEM((stations, windows, segments), jnp.int32),
             pltpu.VMEM((RANK, lags), F32),
             pltpu.VMEM((stations, block, 2, freq), BF16),
-            pltpu.VMEM((2, stations, 2, block, freq // 2), BF16),
-            pltpu.VMEM((2, 2, stations // 2, 2, block, freq // 2), BF16),
+            pltpu.VMEM((CUTS, stations, 2, block, freq // CUTS), BF16),
+            pltpu.VMEM((CUTS, 2, stations // 2, 2, block, freq // CUTS), BF16),
             pltpu.SMEM((2, stations // 2), jnp.int32),
             pltpu.SMEM((2, stations // 2), jnp.int32),
             pltpu.SMEM((2, pairs), jnp.int32),
-            pltpu.VMEM((2 * stations, 2, block, freq // 2), BF16),
-            pltpu.VMEM((2 * stations, 2, block, freq // 2), BF16),
+            pltpu.VMEM((2 * stations, 2, block, freq // CUTS), BF16),
+            pltpu.VMEM((2 * stations, 2, block, freq // CUTS), BF16),
+            pltpu.VMEM((2 * stations, 2, block, freq // CUTS), BF16),
+            pltpu.VMEM((2 * stations, 2, block, freq // CUTS), BF16),
             pltpu.VMEM((2 * count, 2 * freq), BF16),
             pltpu.VMEM((2 * count, half), F32),
             pltpu.VMEM((2 * freq, half), BF16),
@@ -526,8 +532,8 @@
             pltpu.VMEM((2 * chips - 1, 1, 128), F32),
             pltpu.SemaphoreType.DMA((2,)),
             pltpu.SemaphoreType.DMA((2,)),
-            pltpu.SemaphoreType.DMA((2, 2, stations // 2)),
-            pltpu.SemaphoreType.DMA((2, 2, stations // 2)),
+            pltpu.SemaphoreType.DMA((CUTS, 2, stations // 2)),
+            pltpu.SemaphoreType.DMA((CUTS, 2, stations // 2)),
             pltpu.SemaphoreType.DMA((1,)),
             pltpu.SemaphoreType.DMA((1,)),
             pltpu.SemaphoreType.DMA((5,)),

time: 41.4 us -> 41.8 us (level)
  no operation moved by 1% of the time
where the time goes in v11:
time: 41.8 us; the launch traced here: 41.7 us
  Pallas kernels  41 us (98%)
  between operations  0.64 us (2%)
    pallas_call x1, Pallas kernels, on_device(): pl.pallas_call(functools.partial(station_kernel, stations, segments, wind...  40.3 us

profile of v11, /device:TPU:1, one launch (start us, length us, event | category | flops | bytes accessed | tf_op | source)
XLA Modules:
  0.0 41.7 jit_solution(15080531348460351690)
XLA Ops:
  0.6 40.3 %station_pairs.1 = (f32[24,2048]{1,0:T(8,128)S(1)}, f32[2,32,64]{2,1,0:T(8,128)S(1)}) custom-call(s32[2,12]{1,0:T(2,128)} %bitcast.3, s32[8,2,8]{2,1,0:T(2,128)} %masks_hbm.1, bf16[8,16,2,1024]{3,2,1,0:T(2,128)(2,1)} %bitcast.2, bf16[2048,1024]{1,0:T(8,128)(2,1)} %constant.2.clone.table_ref, f32[4,2048]{1,0:T(4,128)} %start_hbm.1), custom_call_target="tpu_custom_call" | custom-call | tf_op jit(solution)/shard_map/station_pairs/pallas_call | solution.py:495
  40.9 0.7 %outputs.1 = (f32[12,2,2048]{2,1,0:T(2,128)}, f32[12,64]{1,0:T(8,128)}, f32[12,4,64]{2,1,0:T(4,128)}) custom-call(f32[24,2048]{1,0:T(8,128)S(1)} %get-tuple-element.5.windows_ref, f32[2,32,64]{2,1,0:T(8,128)S(1)} %get-tuple-element.6.merged_ref), custom_call_target="tpu_custom_call" | custom-call | tf_op jit(solution)/shard_map/outputs/pallas_call | solution.py:551
